TPU v7x, 512 devices: a whole 4x4x16 slice. The times are simulated.
512 devices in a mesh: dp: 32 (over y, z_lo), tensor: 16 (over z_hi, x, core).
Axes of the slice: x: 4, y: 4, z: 16 (z_hi: 2, z_lo: 8; z = z_hi * 8 + z_lo), core: 2. Of those that a mesh axis runs over, the one named last changes fastest.
Arguments:
- output_gradient: bfloat16 [12288, 8192], P(('dp', 'tensor')), may hold values from -6 to 6
- attention_output: bfloat16 [12288, 8192], P('dp', 'tensor'), may hold values from -0.29882812 to 0.29882812
- frozen_projection: bfloat16 [8192, 8192], P('tensor', 'dp'), may hold values from -0.0625 to 0.0625
- domain_down_map: bfloat16 [4, 32, 8192], P(None, None, 'tensor'), may hold values from -0.29882812 to 0.29882812
- domain_up_map: bfloat16 [4, 32, 8192], P(None, None, 'tensor'), may hold values from -0.0625 to 0.0625
- common_down_map: bfloat16 [16, 8192], P(None, 'tensor'), may hold values from -0.29882812 to 0.29882812
- common_up_map: bfloat16 [16, 8192], P(None, 'tensor'), may hold values from -0.0625 to 0.0625
- live_token_count: int32 [32], P('dp'), may hold values from 128 to 384, as said below
- series_domain: int32 [32], replicated, may hold values from 0 to 3, as said below
Outputs:
- grad_input: bfloat16 [12288, 8192], P('dp', 'tensor')
- domain_down_gradient: float32 [4, 32, 8192], P(None, None, 'tensor')
- domain_up_gradient: float32 [4, 32, 8192], P(None, None, 'tensor')
- common_down_gradient: float32 [16, 8192], P(None, 'tensor')
- common_up_gradient: float32 [16, 8192], P(None, 'tensor')
Inputs may be any that keep to these rules, and one draw needn't show every extreme that they name: `live_token_count`: a multiple of 128; some series has exactly 384. `series_domain`: every domain is named by at least one series.
All inputs are finite; a program needn't handle non-finite values.
Results may differ from a plain program's by a relative error of at most 0.0035.
Values may be sent and summed in bfloat16 or wider, within the bound.
No kernel may reach another device: no remote copies, remote signals or barrier semaphores. Data moves between devices by JAX's collectives and lax.ppermute only.
A program may use at most 64 MiB of HBM per device.

v0:
```python
import jax
import jax.numpy as jnp
import numpy as np
from jax import lax
from jax.experimental import pallas as pl
from jax.experimental.pallas import tpu as pltpu
from jax.sharding import Mesh
from jax.sharding import PartitionSpec as P


adapter_scale = 2.0
AXES = ("y", "zl", "zh", "x", "c")
SIZES = (4, 8, 2, 4, 2)
f32 = jnp.float32
bf16 = jnp.bfloat16
NT = (((1,), (1,)), ((), ()))
NN = (((1,), (0,)), ((), ()))
TN = (((0,), (0,)), ((), ()))


def dot(a, b, dims):
    return lax.dot_general(a, b, dims, preferred_element_type=f32)


def exchange(blocks, axis):
    return lax.all_to_all(blocks, axis, 0, 0, tiled=True)


def to_all(block, axis):
    n = lax.axis_size(axis)
    return exchange(jnp.broadcast_to(block[None], (n, *block.shape)), axis)


def shifted(x, axis, step):
    n = lax.axis_size(axis)
    return lax.ppermute(x, axis, [(i, (i + step) % n) for i in range(n)])


def around(x, axis):
    return [x] + [shifted(x, axis, k) for k in range(1, lax.axis_size(axis))]


def picked(blocks, index):
    return lax.dynamic_index_in_dim(blocks, index, 0, keepdims=False)


def ordered_by(test, a, b):
    return [jnp.where(test, a, b), jnp.where(test, b, a)]


def across(x):
    return lax.ppermute(x, "zh", [(0, 1), (1, 0)])


def matmul_kernel(halves, g_ref, w_ref, *o_refs):
    w = jnp.concatenate([w_ref[i] for i in range(w_ref.shape[0])], axis=1)
    rows = o_refs[0].shape[0]
    for i, o_ref in enumerate(o_refs):
        o_ref[...] = dot(g_ref[pl.ds(i * rows, rows), :], w, NT).astype(o_ref.dtype)


def quarter_product(g, w, halves, width, parts):
    rows, depth = g.shape
    planes, heads, block = w.shape
    planes, steps = planes // 2, heads // width
    out = jax.ShapeDtypeStruct((rows // parts, 2 * heads), bf16)
    out_spec = pl.BlockSpec((rows // parts, width), lambda i, h: (0, i))
    return pl.pallas_call(
        matmul_kernel,
        out_shape=[out] * parts,
        grid_spec=pltpu.PrefetchScalarGridSpec(
            num_scalar_prefetch=1,
            grid=(2 * steps,),
            in_specs=[
                pl.BlockSpec((rows, depth), lambda i, h: (0, 0)),
                pl.BlockSpec(
                    (planes, width, block),
                    lambda i, h: (h[lax.div(i, steps)], lax.rem(i, steps), 0),
                ),
            ],
            out_specs=[out_spec] * parts,
        ),
        cost_estimate=pl.CostEstimate(
            flops=4 * rows * depth * heads,
            bytes_accessed=2 * (rows * depth + 2 * heads * depth + 2 * rows * heads),
            transcendentals=0,
        ),
        name="quarter_product",
    )(halves, g, w)


def on_device(
    output_gradient,
    attention_output,
    frozen_projection,
    domain_down_map,
    domain_up_map,
    common_down_map,
    common_up_map,
    live_token_count,
    series_domain,
):
    rows, width = output_gradient.shape
    heads = attention_output.shape[1]
    ny, nzl, nx, nc = (lax.axis_size(a) for a in ("y", "zl", "x", "c"))
    nxc = nx * nc
    y, zl, zh, x, c = (lax.axis_index(a) for a in AXES)
    domains, rank, _ = domain_down_map.shape
    shared = common_down_map.shape[0]
    low = rank + shared
    half_rows = nxc * rows

    planes = lax.all_gather(frozen_projection, ("zh", "zl"), axis=0)

    positions = ((zh * nx + x) * nc + c) * rows + lax.iota(jnp.int32, rows)
    live = (positions < live_token_count[0])[:, None]
    masked = jnp.where(live, output_gradient, jnp.zeros_like(output_gradient))

    quarter = width // ny
    domain = lax.dynamic_index_in_dim(series_domain, y * nzl + zl, 0, keepdims=False)
    up = jnp.concatenate([picked(domain_up_map, domain), common_up_map])
    down = jnp.concatenate([picked(domain_down_map, domain), common_down_map])
    first = zh == 0

    def here(x):
        return jnp.where(first, x[:, : x.shape[1] // 2], x[:, x.shape[1] // 2 :])

    def there(x):
        return jnp.where(first, x[:, x.shape[1] // 2 :], x[:, : x.shape[1] // 2])

    labels = lax.dynamic_slice_in_dim(series_domain.reshape(ny, nzl), zl, 1, axis=1)
    picker = (labels == lax.iota(jnp.int32, domains)[None, :]).astype(f32)
    low_part = dot(down, attention_output, NT)
    low_away = there(low_part)
    low_high = lax.reduce_precision(low_away, 8, 7)
    low_rest = (low_away - low_high).astype(bf16)
    far = across(jnp.concatenate([up, low_high.astype(bf16), low_rest], axis=1))
    cols = masked.reshape(rows, 2, nxc, heads).transpose(2, 0, 1, 3)
    cols = exchange(cols.reshape(nxc, rows, 2 * heads), ("x", "c"))
    g = []
    for k in range(ny):
        at = lax.rem(y + k, ny) * quarter
        block = lax.dynamic_slice_in_dim(masked, at, quarter, axis=1)
        g.append(shifted(block, "y", k) if k else block)
    g = jnp.stack(g)
    cols = cols.reshape(half_rows, 2 * heads)
    far_up, far_low = far[:, :heads], far[:, heads:].astype(f32)
    low_part = here(low_part) + far_low[:, :half_rows] + far_low[:, half_rows:]
    back_part = dot(jnp.concatenate(ordered_by(first, up, far_up), axis=1), cols, NT)
    sums = to_all(jnp.concatenate([back_part, low_part], axis=1), ("x", "c"))
    g = jnp.stack(around(g.reshape(ny * rows, quarter), "x"))
    sums = sums.sum(0).astype(bf16)
    back_own, low_own = sums[:, :half_rows], sums[:, half_rows:]
    far = across(jnp.concatenate([back_own, down], axis=1))
    up_grad = adapter_scale * dot(low_own, cols, NN)
    other = shifted(g, "c", 1)
    far, other, up_grad = lax.optimization_barrier((far, other, up_grad))
    back_far, far_down = far[:, :half_rows], far[:, half_rows:]
    back_all = jnp.concatenate(ordered_by(first, back_own, back_far), axis=1)
    down_grad = adapter_scale * dot(back_all, attention_output, NN)
    piece = heads // ny
    grads = jnp.stack(
        [
            jnp.concatenate(
                [
                    m[:, at + i * piece : at + (i + 1) * piece]
                    for m, at in ((down_grad, 0), (up_grad, 0), (up_grad, heads))
                ]
            )
            for i in range(ny)
        ]
    )
    grads = exchange(grads, "y")

    pair = jnp.stack(ordered_by(c == 0, g, other), axis=1)
    g = jnp.stack([picked(pair, lax.rem(x - i + nx, nx)) for i in range(nx)])
    g = g.reshape(nx, nc, ny, rows, quarter).transpose(2, 0, 1, 3, 4)
    g = g.reshape(ny * half_rows, quarter)

    g, grads = lax.optimization_barrier((g, grads))
    grads = grads.reshape(ny, 3, low, piece)
    own = (picker[:, None, :, None, None] * grads[:, :, None, :rank, :]).sum(0)
    common = grads[:, :, rank:, :].sum(0)
    dom, lines = domains * rank, 2 * (domains * rank + shared)
    spare = -lines % (8 * nzl)
    full = jnp.concatenate([own.reshape(3, dom, piece), common], axis=1)
    full = full.reshape(3, lines // 2, piece)
    blocks = []
    for h in range(2):
        blocks += [jnp.where(zh == h, full[0], jnp.zeros_like(full[0])), full[1 + h]]
    packed = jnp.pad(jnp.stack(blocks).reshape(2, lines, piece), ((0, 0), (0, spare), (0, 0)))
    lines = lines + spare
    packed = packed.reshape(2 * nzl, lines // nzl, piece)
    packed = exchange(packed, ("zh", "zl")).sum(0)
    packed = to_all(packed, "zl").reshape(lines, piece)
    packed = to_all(packed, "y")
    packed = jnp.concatenate([packed[i] for i in range(ny)], axis=1)
    grads = packed[: 2 * (dom + shared)].reshape(2, dom + shared, heads)
    domain_down_gradient, domain_up_gradient = grads[:, :dom].reshape(2, domains, rank, heads)
    common_down_gradient, common_up_gradient = grads[:, dom:]

    parts = quarter_product(g, planes, jnp.stack([1 - zh, zh]), 256, ny)
    parts = [shifted(parts[k], "y", -k) if k else parts[k] for k in range(ny)]

    def finished(at, maps):
        part = sum(p[:, at : at + heads].astype(f32) for p in parts)
        return (part + adapter_scale * dot(back_own, maps, TN)).astype(bf16)

    far_out = across(finished(0, far_down))
    own_out = finished(heads, down)
    grad_input = jnp.concatenate(ordered_by(first, own_out, far_out))
    return (
        grad_input,
        domain_down_gradient,
        domain_up_gradient,
        common_down_gradient,
        common_up_gradient,
    )


def solution(mesh):
    inner = Mesh(np.asarray(mesh.devices).reshape(SIZES), AXES)
    dp, tensor = ("y", "zl"), ("zh", "x", "c")

    return jax.shard_map(
        on_device,
        mesh=inner,
        in_specs=(
            P(dp + tensor, None),
            P(dp, tensor),
            P(tensor, dp),
            P(None, None, tensor),
            P(None, None, tensor),
            P(None, tensor),
            P(None, tensor),
            P(dp),
            P(),
        ),
        out_specs=(
            P(dp, tensor),
            P(None, None, tensor),
            P(None, None, tensor),
            P(None, tensor),
            P(None, tensor),
        ),
        check_vma=False,
    )
```

profile of v0, /device:TPU:78, one launch (start us, length us, event | category | flops | bytes accessed | tf_op | source)
XLA Modules:
  0.0 230.6 jit_solution(1150293716425384215)
XLA Ops:
  8.0 1.1 broadcast_select_fusion
  9.2 2.4 %collective-permute-start.2 = (bf16[24,2048]{1,0:T(8,128)(2,1)S(1)}, bf16[24,2048]{1,0:T(8,128)(2,1)S(1)}, u32[]{:S(2)}, u32[]{:S(2)}) collective-permute-start(bf16[24,2048]{1,0:T(8,128)(2,1)S(1)} %get-tuple-element.40), channel_id=1, source_target_pairs={{0,384},{128,0},{256,128},{384,256},{1,385},{129,1},{257,129},{385... | collective-permute-start | bytes 294920 | tf_op jit(solution)/shard_map/ppermute | solution.py:36
  11.5 4.5 %collective-permute-start.1 = (bf16[24,2048]{1,0:T(8,128)(2,1)S(1)}, bf16[24,2048]{1,0:T(8,128)(2,1)S(1)}, u32[]{:S(2)}, u32[]{:S(2)}) collective-permute-start(bf16[24,2048]{1,0:T(8,128)(2,1)S(1)} %get-tuple-element.41), channel_id=1, source_target_pairs={{0,256},{128,384},{256,0},{384,128},{1,257},{129,385},{257,1},{385... | collective-permute-start | bytes 294920 | tf_op jit(solution)/shard_map/ppermute | solution.py:36
  16.0 3.8 %collective-permute-start = (bf16[24,2048]{1,0:T(8,128)(2,1)S(1)}, bf16[24,2048]{1,0:T(8,128)(2,1)S(1)}, u32[]{:S(2)}, u32[]{:S(2)}) collective-permute-start(bf16[24,2048]{1,0:T(8,128)(2,1)S(1)} %get-tuple-element.42), channel_id=1, source_target_pairs={{0,128},{128,256},{256,384},{384,0},{1,129},{129,257},{257,385},{3... | collective-permute-start | bytes 294920 | tf_op jit(solution)/shard_map/ppermute | solution.py:36
  19.9 0.6 dynamic_slice.43
  22.4 0.8 dynamic-slice_bitcast_fusion.1
  23.7 2.7 %collective-permute-start.5 = (bf16[96,2048]{1,0:T(8,128)(2,1)S(1)}, bf16[96,2048]{1,0:T(8,128)(2,1)S(1)}, u32[]{:S(2)}, u32[]{:S(2)}) collective-permute-start(bf16[96,2048]{1,0:T(8,128)(2,1)S(1)} %bitcast.70), channel_id=1, source_target_pairs={{0,6},{2,0},{4,2},{6,4},{1,7},{3,1},{5,3},{7,5},{8,14},{10,8},{12,... | collective-permute-start | bytes 1179656 | tf_op jit(solution)/shard_map/ppermute | solution.py:36
  26.4 3.0 %collective-permute-start.4 = (bf16[96,2048]{1,0:T(8,128)(2,1)S(1)}, bf16[96,2048]{1,0:T(8,128)(2,1)S(1)}, u32[]{:S(2)}, u32[]{:S(2)}) collective-permute-start(bf16[96,2048]{1,0:T(8,128)(2,1)S(1)} %bitcast.71), channel_id=1, source_target_pairs={{0,4},{2,6},{4,0},{6,2},{1,5},{3,7},{5,1},{7,3},{8,12},{10,14},{12... | collective-permute-start | bytes 1179656 | tf_op jit(solution)/shard_map/ppermute | solution.py:36
  29.4 4.0 %collective-permute-start.3 = (bf16[96,2048]{1,0:T(8,128)(2,1)S(1)}, bf16[96,2048]{1,0:T(8,128)(2,1)S(1)}, u32[]{:S(2)}, u32[]{:S(2)}) collective-permute-start(bf16[96,2048]{1,0:T(8,128)(2,1)S(1)} %bitcast.72), channel_id=1, source_target_pairs={{0,2},{2,4},{4,6},{6,0},{1,3},{3,5},{5,7},{7,1},{8,10},{10,12},{12... | collective-permute-start | bytes 1179656 | tf_op jit(solution)/shard_map/ppermute | solution.py:36
  33.5 13.9 %collective-permute-start.6 = (bf16[48,896]{1,0:T(8,128)(2,1)S(1)}, bf16[48,896]{1,0:T(8,128)(2,1)S(1)}, u32[]{:S(2)}, u32[]{:S(2)}) collective-permute-start(bf16[48,896]{1,0:T(8,128)(2,1)S(1)} %pad_maximum_fusion.8), channel_id=1, source_target_pairs={{0,8},{8,0},{1,9},{9,1},{2,10},{10,2},{3,11},{11,3},{4,12},{12,4},... | collective-permute-start | bytes 258056 | tf_op jit(solution)/shard_map/ppermute | solution.py:52
  47.6 0.3 copy.22
  47.9 1.0 reshape.84
  48.9 4.5 %all-to-all-start = ((bf16[8,24,1024]{2,1,0:T(8,128)(2,1)}), bf16[8,24,1024]{2,1,0:T(8,128)(2,1)S(1)}, u32[]{:S(2)}, u32[]{:S(2)}) async-start(bf16[8,24,1024]{2,1,0:T(8,128)(2,1)} %reshape.84), calls=%async_computation | async-start | bytes 786432 | tf_op jit(solution)/shard_map/all_to_all | solution.py:26
  53.4 0.5 collective-permute-done.6
  54.0 1.4 pad_maximum_fusion.1
  55.3 1.9 collective-permute-start.8
  57.4 2.9 %all-to-all-done = bf16[8,24,1024]{2,1,0:T(8,128)(2,1)S(1)} async-done(((bf16[8,24,1024]{2,1,0:T(8,128)(2,1)}), bf16[8,24,1024]{2,1,0:T(8,128)(2,1)S(1)}, u32[]{:S(2)}, u32[]{:S(2)}) %all-to-all-start) | async-done | bytes 393248 | tf_op jit(solution)/shard_map/all_to_all | solution.py:26
  60.6 0.9 broadcast_in_dim.20
  61.5 5.5 %all-to-all-start.1 = ((f32[8,48,384]{2,1,0:T(8,128)}), f32[8,48,384]{2,1,0:T(8,128)S(1)}, u32[]{:S(2)}, u32[]{:S(2)}) async-start(f32[8,48,384]{2,1,0:T(8,128)} %broadcast_in_dim.20), calls=%async_computation.1 | async-start | bytes 1179648 | tf_op jit(solution)/shard_map/all_to_all | solution.py:26
  67.4 8.6 %all-to-all-done.1 = f32[8,48,384]{2,1,0:T(8,128)S(1)} async-done(((f32[8,48,384]{2,1,0:T(8,128)}), f32[8,48,384]{2,1,0:T(8,128)S(1)}, u32[]{:S(2)}, u32[]{:S(2)}) %all-to-all-start.1) | async-done | bytes 589856 | tf_op jit(solution)/shard_map/all_to_all | solution.py:26
  76.1 10.7 %collective-permute-start.7 = (bf16[48,704]{1,0:T(8,128)(2,1)S(1)}, bf16[48,704]{1,0:T(8,128)(2,1)S(1)}, u32[]{:S(2)}, u32[]{:S(2)}) collective-permute-start(bf16[48,704]{1,0:T(8,128)(2,1)S(1)} %maximum_maximum_fusion), channel_id=1, source_target_pairs={{0,8},{8,0},{1,9},{9,1},{2,10},{10,2},{3,11},{11,3},{4,12},{12,4},... | collective-permute-start | bytes 202760 | tf_op jit(solution)/shard_map/ppermute | solution.py:52
  87.1 9.8 %collective-permute-done.7 = bf16[48,704]{1,0:T(8,128)(2,1)S(1)} collective-permute-done((bf16[48,704]{1,0:T(8,128)(2,1)S(1)}, bf16[48,704]{1,0:T(8,128)(2,1)S(1)}, u32[]{:S(2)}, u32[]{:S(2)}) %collective-permute-start.7) | collective-permute-done | bytes 67616 | tf_op jit(solution)/shard_map/ppermute | solution.py:52
  97.3 0.7 pad_maximum_fusion.7
  98.0 5.0 %all-to-all-start.2 = ((f32[4,144,128]{2,1,0:T(8,128)}), f32[4,144,128]{2,1,0:T(8,128)S(1)}, u32[]{:S(2)}, u32[]{:S(2)}) async-start(f32[4,144,128]{2,1,0:T(8,128)} %pad_maximum_fusion.7), calls=%async_computation.2 | async-start | bytes 589824 | tf_op jit(solution)/shard_map/all_to_all | solution.py:26
  103.0 1.7 select_bitcast_fusion
  104.7 0.3 fusion.1
  105.0 0.4 pad_maximum_fusion
  105.4 2.1 copy.19
  107.5 0.9 all-to-all-done.2
  108.6 29.8 %all_to_all.30 = f32[16,40,128]{2,1,0:T(8,128)S(1)} all-to-all(f32[16,40,128]{2,1,0:T(8,128)S(1)} %bitcast.91), channel_id=1, replica_groups=mesh['y'=4,'zl'=8,'zh'=2,'x'=4,'c'=2] {'zh','zl'}, dimensions={0} | all-to-all | bytes 655360 | tf_op jit(solution)/shard_map/all_to_all | solution.py:26
  138.5 16.7 %all_to_all.31 = f32[8,40,128]{2,1,0:T(8,128)S(1)} all-to-all(f32[8,40,128]{2,1,0:T(8,128)S(1)} %broadcast_in_dim.21), channel_id=1, replica_groups=mesh['y'=4,'zl'=8,'zh'=2,'x'=4,'c'=2] {'zl'}, dimensions={0} | all-to-all | bytes 327680 | tf_op jit(solution)/shard_map/all_to_all | solution.py:26
  155.2 0.9 broadcast_in_dim.39
  156.1 4.9 %all-to-all-start.5 = ((f32[4,320,128]{2,1,0:T(8,128)}), f32[4,320,128]{2,1,0:T(8,128)S(1)}, u32[]{:S(2)}, u32[]{:S(2)}) async-start(f32[4,320,128]{2,1,0:T(8,128)} %broadcast_in_dim.39), calls=%async_computation.5 | async-start | bytes 1310720 | tf_op jit(solution)/shard_map/all_to_all | solution.py:26
  161.0 0.6 pad_add_fusion.halves
  161.6 9.7 %quarter_product.1 = (bf16[192,1024]{1,0:T(8,128)(2,1)}, bf16[192,1024]{1,0:T(8,128)(2,1)}, bf16[192,1024]{1,0:T(8,128)(2,1)}, bf16[192,1024]{1,0:T(8,128)(2,1)}) custom-call(s32[2]{0:T(128)} %pad_add_fusion.halves, bf16[768,2048]{1,0:T(8,128)(2,1)} %bitcast.78, bf16[16,512,256]{2,1,0:T(8,128)(2,1)} %bitcast.101), custom_call_target="tpu_custom_call" | custom-call | flops 3221225472 | bytes 8912896 | tf_op jit(solution)/shard_map/quarter_product/pallas_call | solution.py:68
  171.3 3.4 %collective-permute-start.11 = (bf16[192,1024]{1,0:T(8,128)(2,1)}, bf16[192,1024]{1,0:T(8,128)(2,1)S(1)}, u32[]{:S(2)}, u32[]{:S(2)}) collective-permute-start(bf16[192,1024]{1,0:T(8,128)(2,1)} %get-tuple-element.21), channel_id=1, source_target_pairs={{0,128},{128,256},{256,384},{384,0},{1,129},{129,257},{257,385},{3... | collective-permute-start | bytes 1179656 | tf_op jit(solution)/shard_map/ppermute | solution.py:36
  174.7 2.6 %collective-permute-start.10 = (bf16[192,1024]{1,0:T(8,128)(2,1)}, bf16[192,1024]{1,0:T(8,128)(2,1)S(1)}, u32[]{:S(2)}, u32[]{:S(2)}) collective-permute-start(bf16[192,1024]{1,0:T(8,128)(2,1)} %get-tuple-element.20), channel_id=1, source_target_pairs={{0,256},{128,384},{256,0},{384,128},{1,257},{129,385},{257,1},{385... | collective-permute-start | bytes 1179656 | tf_op jit(solution)/shard_map/ppermute | solution.py:36
  177.3 4.6 %collective-permute-start.9 = (bf16[192,1024]{1,0:T(8,128)(2,1)}, bf16[192,1024]{1,0:T(8,128)(2,1)S(1)}, u32[]{:S(2)}, u32[]{:S(2)}) collective-permute-start(bf16[192,1024]{1,0:T(8,128)(2,1)} %get-tuple-element.19), channel_id=1, source_target_pairs={{0,384},{128,0},{256,128},{384,256},{1,385},{129,1},{257,129},{385... | collective-permute-start | bytes 1179656 | tf_op jit(solution)/shard_map/ppermute | solution.py:36
  182.0 0.8 fusion.26
  182.8 2.6 %collective-permute-done.11 = bf16[192,1024]{1,0:T(8,128)(2,1)S(1)} collective-permute-done((bf16[192,1024]{1,0:T(8,128)(2,1)}, bf16[192,1024]{1,0:T(8,128)(2,1)S(1)}, u32[]{:S(2)}, u32[]{:S(2)}) %collective-permute-start.11) | collective-permute-done | bytes 393248 | tf_op jit(solution)/shard_map/ppermute | solution.py:36
  185.4 4.9 %collective-permute-done.10 = bf16[192,1024]{1,0:T(8,128)(2,1)S(1)} collective-permute-done((bf16[192,1024]{1,0:T(8,128)(2,1)}, bf16[192,1024]{1,0:T(8,128)(2,1)S(1)}, u32[]{:S(2)}, u32[]{:S(2)}) %collective-permute-start.10) | collective-permute-done | bytes 393248 | tf_op jit(solution)/shard_map/ppermute | solution.py:36
  190.3 4.8 %collective-permute-done.9 = bf16[192,1024]{1,0:T(8,128)(2,1)S(1)} collective-permute-done((bf16[192,1024]{1,0:T(8,128)(2,1)}, bf16[192,1024]{1,0:T(8,128)(2,1)S(1)}, u32[]{:S(2)}, u32[]{:S(2)}) %collective-permute-start.9) | collective-permute-done | bytes 393248 | tf_op jit(solution)/shard_map/ppermute | solution.py:36
  195.1 0.3 add_convert_fusion
  195.3 4.9 %collective-permute-start.12 = (bf16[192,512]{1,0:T(8,128)(2,1)S(1)}, bf16[192,512]{1,0:T(8,128)(2,1)S(1)}, u32[]{:S(2)}, u32[]{:S(2)}) collective-permute-start(bf16[192,512]{1,0:T(8,128)(2,1)S(1)} %add_convert_fusion), channel_id=1, source_target_pairs={{0,8},{8,0},{1,9},{9,1},{2,10},{10,2},{3,11},{11,3},{4,12},{12,4},... | collective-permute-start | bytes 589832 | tf_op jit(solution)/shard_map/ppermute | solution.py:52
  200.3 0.6 slice_bitcast_fusion.4
  200.9 21.8 %collective-permute-done.12 = bf16[192,512]{1,0:T(8,128)(2,1)S(1)} collective-permute-done((bf16[192,512]{1,0:T(8,128)(2,1)S(1)}, bf16[192,512]{1,0:T(8,128)(2,1)S(1)}, u32[]{:S(2)}, u32[]{:S(2)}) %collective-permute-start.12) | collective-permute-done | bytes 196640 | tf_op jit(solution)/shard_map/ppermute | solution.py:52
  222.7 0.3 broadcast_select_fusion.2
  222.9 0.8 pad_maximum_fusion.6
  (58 shorter events, 2.5 us)
Async XLA Ops:
  7.2 16.0 %copy-start = (bf16[384,512]{1,0:T(8,128)(2,1)S(1)}, bf16[384,512]{1,0:T(8,128)(2,1)}, u32[]{:S(2)}) copy-start(bf16[384,512]{1,0:T(8,128)(2,1)} %param.10) | copy-start | bytes 1179652
  7.2 12.7 %copy-start.3 = (s32[32]{0:T(128)S(1)}, s32[32]{0:T(128)}, u32[]{:S(2)}) copy-start(s32[32]{0:T(128)} %param.17) | copy-start | bytes 388
  7.2 16.0 %copy-start.2 = (bf16[16,512]{1,0:T(8,128)(2,1)S(1)}, bf16[16,512]{1,0:T(8,128)(2,1)}, u32[]{:S(2)}) copy-start(bf16[16,512]{1,0:T(8,128)(2,1)} %param.14) | copy-start | bytes 49156
  7.2 154.4 %all-gather.3.cloned.1.call-start = ((), (), s32[]{:S(2)}) async-start(), calls=%async_computation.6 | async-start | bytes 4456448 | tf_op jit(solution)/shard_map/all_gather | solution.py:113
  8.0 25.5 %copy-start.1 = (bf16[16,512]{1,0:T(8,128)(2,1)S(1)}, bf16[16,512]{1,0:T(8,128)(2,1)}, u32[]{:S(2)}) copy-start(bf16[16,512]{1,0:T(8,128)(2,1)} %param.15) | copy-start | bytes 49156
  9.2 14.4 %collective-permute-start.2 = (bf16[24,2048]{1,0:T(8,128)(2,1)S(1)}, bf16[24,2048]{1,0:T(8,128)(2,1)S(1)}, u32[]{:S(2)}, u32[]{:S(2)}) collective-permute-start(bf16[24,2048]{1,0:T(8,128)(2,1)S(1)} %get-tuple-element.40), channel_id=1, source_target_pairs={{0,384},{128,0},{256,128},{384,256},{1,385},{129,1},{257,129},{385... | collective-permute-start | bytes 294920 | tf_op jit(solution)/shard_map/ppermute | solution.py:36
  11.5 12.1 %collective-permute-start.1 = (bf16[24,2048]{1,0:T(8,128)(2,1)S(1)}, bf16[24,2048]{1,0:T(8,128)(2,1)S(1)}, u32[]{:S(2)}, u32[]{:S(2)}) collective-permute-start(bf16[24,2048]{1,0:T(8,128)(2,1)S(1)} %get-tuple-element.41), channel_id=1, source_target_pairs={{0,256},{128,384},{256,0},{384,128},{1,257},{129,385},{257,1},{385... | collective-permute-start | bytes 294920 | tf_op jit(solution)/shard_map/ppermute | solution.py:36
  16.0 7.6 %collective-permute-start = (bf16[24,2048]{1,0:T(8,128)(2,1)S(1)}, bf16[24,2048]{1,0:T(8,128)(2,1)S(1)}, u32[]{:S(2)}, u32[]{:S(2)}) collective-permute-start(bf16[24,2048]{1,0:T(8,128)(2,1)S(1)} %get-tuple-element.42), channel_id=1, source_target_pairs={{0,128},{128,256},{256,384},{384,0},{1,129},{129,257},{257,385},{3... | collective-permute-start | bytes 294920 | tf_op jit(solution)/shard_map/ppermute | solution.py:36
  23.7 30.3 %collective-permute-start.5 = (bf16[96,2048]{1,0:T(8,128)(2,1)S(1)}, bf16[96,2048]{1,0:T(8,128)(2,1)S(1)}, u32[]{:S(2)}, u32[]{:S(2)}) collective-permute-start(bf16[96,2048]{1,0:T(8,128)(2,1)S(1)} %bitcast.70), channel_id=1, source_target_pairs={{0,6},{2,0},{4,2},{6,4},{1,7},{3,1},{5,3},{7,5},{8,14},{10,8},{12,... | collective-permute-start | bytes 1179656 | tf_op jit(solution)/shard_map/ppermute | solution.py:36
  26.4 27.5 %collective-permute-start.4 = (bf16[96,2048]{1,0:T(8,128)(2,1)S(1)}, bf16[96,2048]{1,0:T(8,128)(2,1)S(1)}, u32[]{:S(2)}, u32[]{:S(2)}) collective-permute-start(bf16[96,2048]{1,0:T(8,128)(2,1)S(1)} %bitcast.71), channel_id=1, source_target_pairs={{0,4},{2,6},{4,0},{6,2},{1,5},{3,7},{5,1},{7,3},{8,12},{10,14},{12... | collective-permute-start | bytes 1179656 | tf_op jit(solution)/shard_map/ppermute | solution.py:36
  29.4 24.5 %collective-permute-start.3 = (bf16[96,2048]{1,0:T(8,128)(2,1)S(1)}, bf16[96,2048]{1,0:T(8,128)(2,1)S(1)}, u32[]{:S(2)}, u32[]{:S(2)}) collective-permute-start(bf16[96,2048]{1,0:T(8,128)(2,1)S(1)} %bitcast.72), channel_id=1, source_target_pairs={{0,2},{2,4},{4,6},{6,0},{1,3},{3,5},{5,7},{7,1},{8,10},{10,12},{12... | collective-permute-start | bytes 1179656 | tf_op jit(solution)/shard_map/ppermute | solution.py:36
  33.5 20.4 %collective-permute-start.6 = (bf16[48,896]{1,0:T(8,128)(2,1)S(1)}, bf16[48,896]{1,0:T(8,128)(2,1)S(1)}, u32[]{:S(2)}, u32[]{:S(2)}) collective-permute-start(bf16[48,896]{1,0:T(8,128)(2,1)S(1)} %pad_maximum_fusion.8), channel_id=1, source_target_pairs={{0,8},{8,0},{1,9},{9,1},{2,10},{10,2},{3,11},{11,3},{4,12},{12,4},... | collective-permute-start | bytes 258056 | tf_op jit(solution)/shard_map/ppermute | solution.py:52
  48.9 11.4 %all-to-all-start = ((bf16[8,24,1024]{2,1,0:T(8,128)(2,1)}), bf16[8,24,1024]{2,1,0:T(8,128)(2,1)S(1)}, u32[]{:S(2)}, u32[]{:S(2)}) async-start(bf16[8,24,1024]{2,1,0:T(8,128)(2,1)} %reshape.84), calls=%async_computation | async-start | bytes 786432 | tf_op jit(solution)/shard_map/all_to_all | solution.py:26
  55.3 41.6 %collective-permute-start.8 = (bf16[4,96,2048]{2,1,0:T(8,128)(2,1)}, bf16[4,96,2048]{2,1,0:T(8,128)(2,1)}, u32[]{:S(2)}, u32[]{:S(2)}) collective-permute-start(bf16[4,96,2048]{2,1,0:T(8,128)(2,1)} %pad_maximum_fusion.1), channel_id=1, source_target_pairs={{0,1},{1,0},{2,3},{3,2},{4,5},{5,4},{6,7},{7,6},{8,9},{9,8},{10,11... | collective-permute-start | bytes 4718600 | tf_op jit(solution)/shard_map/ppermute | solution.py:36
  61.5 14.5 %all-to-all-start.1 = ((f32[8,48,384]{2,1,0:T(8,128)}), f32[8,48,384]{2,1,0:T(8,128)S(1)}, u32[]{:S(2)}, u32[]{:S(2)}) async-start(f32[8,48,384]{2,1,0:T(8,128)} %broadcast_in_dim.20), calls=%async_computation.1 | async-start | bytes 1179648 | tf_op jit(solution)/shard_map/all_to_all | solution.py:26
  76.1 20.8 %collective-permute-start.7 = (bf16[48,704]{1,0:T(8,128)(2,1)S(1)}, bf16[48,704]{1,0:T(8,128)(2,1)S(1)}, u32[]{:S(2)}, u32[]{:S(2)}) collective-permute-start(bf16[48,704]{1,0:T(8,128)(2,1)S(1)} %maximum_maximum_fusion), channel_id=1, source_target_pairs={{0,8},{8,0},{1,9},{9,1},{2,10},{10,2},{3,11},{11,3},{4,12},{12,4},... | collective-permute-start | bytes 202760 | tf_op jit(solution)/shard_map/ppermute | solution.py:52
  98.0 10.4 %all-to-all-start.2 = ((f32[4,144,128]{2,1,0:T(8,128)}), f32[4,144,128]{2,1,0:T(8,128)S(1)}, u32[]{:S(2)}, u32[]{:S(2)}) async-start(f32[4,144,128]{2,1,0:T(8,128)} %pad_maximum_fusion.7), calls=%async_computation.2 | async-start | bytes 589824 | tf_op jit(solution)/shard_map/all_to_all | solution.py:26
  156.1 25.8 %all-to-all-start.5 = ((f32[4,320,128]{2,1,0:T(8,128)}), f32[4,320,128]{2,1,0:T(8,128)S(1)}, u32[]{:S(2)}, u32[]{:S(2)}) async-start(f32[4,320,128]{2,1,0:T(8,128)} %broadcast_in_dim.39), calls=%async_computation.5 | async-start | bytes 1310720 | tf_op jit(solution)/shard_map/all_to_all | solution.py:26
  171.3 14.1 %collective-permute-start.11 = (bf16[192,1024]{1,0:T(8,128)(2,1)}, bf16[192,1024]{1,0:T(8,128)(2,1)S(1)}, u32[]{:S(2)}, u32[]{:S(2)}) collective-permute-start(bf16[192,1024]{1,0:T(8,128)(2,1)} %get-tuple-element.21), channel_id=1, source_target_pairs={{0,128},{128,256},{256,384},{384,0},{1,129},{129,257},{257,385},{3... | collective-permute-start | bytes 1179656 | tf_op jit(solution)/shard_map/ppermute | solution.py:36
  174.7 15.6 %collective-permute-start.10 = (bf16[192,1024]{1,0:T(8,128)(2,1)}, bf16[192,1024]{1,0:T(8,128)(2,1)S(1)}, u32[]{:S(2)}, u32[]{:S(2)}) collective-permute-start(bf16[192,1024]{1,0:T(8,128)(2,1)} %get-tuple-element.20), channel_id=1, source_target_pairs={{0,256},{128,384},{256,0},{384,128},{1,257},{129,385},{257,1},{385... | collective-permute-start | bytes 1179656 | tf_op jit(solution)/shard_map/ppermute | solution.py:36
  177.2 17.8 %copy-start.4 = (bf16[192,1024]{1,0:T(8,128)(2,1)S(1)}, bf16[192,1024]{1,0:T(8,128)(2,1)}, u32[]{:S(2)}) copy-start(bf16[192,1024]{1,0:T(8,128)(2,1)} %get-tuple-element.18) | copy-start | bytes 1179652
  177.3 17.8 %collective-permute-start.9 = (bf16[192,1024]{1,0:T(8,128)(2,1)}, bf16[192,1024]{1,0:T(8,128)(2,1)S(1)}, u32[]{:S(2)}, u32[]{:S(2)}) collective-permute-start(bf16[192,1024]{1,0:T(8,128)(2,1)} %get-tuple-element.19), channel_id=1, source_target_pairs={{0,384},{128,0},{256,128},{384,256},{1,385},{129,1},{257,129},{385... | collective-permute-start | bytes 1179656 | tf_op jit(solution)/shard_map/ppermute | solution.py:36
  195.3 27.3 %collective-permute-start.12 = (bf16[192,512]{1,0:T(8,128)(2,1)S(1)}, bf16[192,512]{1,0:T(8,128)(2,1)S(1)}, u32[]{:S(2)}, u32[]{:S(2)}) collective-permute-start(bf16[192,512]{1,0:T(8,128)(2,1)S(1)} %add_convert_fusion), channel_id=1, source_target_pairs={{0,8},{8,0},{1,9},{9,1},{2,10},{10,2},{3,11},{11,3},{4,12},{12,4},... | collective-permute-start | bytes 589832 | tf_op jit(solution)/shard_map/ppermute | solution.py:52
Sparse Core Ops, SparseCore 0:
  20.0 90.0 all-gather.2
where the time goes:
time: 232 us; the launch traced here: 231 us
  starting transfers between devices  82.4 us (36%)
  waiting for transfers between devices  56.7 us (24%)
  blocking collectives  46.5 us (20%)
  between operations  17.2 us (7%)
  Pallas kernels  9.72 us (4%)
  local copies, waits for them, and re-layouts  8.64 us (4%)
  other arithmetic  7.93 us (3%)
    all_to_all x2, blocking collectives, exchange(): return lax.all_to_all(blocks, axis, 0, 0, tiled=True)  46.5 us
    ppermute x10, starting transfers between devices, shifted(): return lax.ppermute(x, axis, [(i, (i + step) % n) for i in range(n)])  32.9 us
    ppermute x3, waiting for transfers between devices, across(): return lax.ppermute(x, 'zh', [(0, 1), (1, 0)])  32.1 us
    ppermute x3, starting transfers between devices, across(): return lax.ppermute(x, 'zh', [(0, 1), (1, 0)])  29.5 us
    all_to_all x4, starting transfers between devices, exchange(): return lax.all_to_all(blocks, axis, 0, 0, tiled=True)  19.9 us
    all_to_all x4, waiting for transfers between devices, exchange(): return lax.all_to_all(blocks, axis, 0, 0, tiled=True)  12.3 us
    ppermute x10, waiting for transfers between devices, shifted(): return lax.ppermute(x, axis, [(i, (i + step) % n) for i in range(n)])  12.2 us
    pallas_call x1, Pallas kernels, quarter_product(): pl.pallas_call(matmul_kernel, out_shape=[out] * parts, grid_spec=pltpu.Pr...  9.72 us
  transfers between devices with their start and end apart: 18, of which 9 were waited for; matrix products, arithmetic and copies ran while one was open for 7% of the time, Pallas kernels for 4%

commit v1 on v0

--- a/solution.py
+++ b/solution.py
@@ -52,41 +52,38 @@
     return lax.ppermute(x, "zh", [(0, 1), (1, 0)])
 
 
-def matmul_kernel(halves, g_ref, w_ref, *o_refs):
+def matmul_kernel(half, g_ref, w_ref, *o_refs):
     w = jnp.concatenate([w_ref[i] for i in range(w_ref.shape[0])], axis=1)
     rows = o_refs[0].shape[0]
     for i, o_ref in enumerate(o_refs):
         o_ref[...] = dot(g_ref[pl.ds(i * rows, rows), :], w, NT).astype(o_ref.dtype)
 
 
-def quarter_product(g, w, halves, width, parts):
+def half_product(g, w, half, width, parts):
     rows, depth = g.shape
     planes, heads, block = w.shape
-    planes, steps = planes // 2, heads // width
-    out = jax.ShapeDtypeStruct((rows // parts, 2 * heads), bf16)
+    planes = planes // 2
+    out = jax.ShapeDtypeStruct((rows // parts, heads), bf16)
     out_spec = pl.BlockSpec((rows // parts, width), lambda i, h: (0, i))
     return pl.pallas_call(
         matmul_kernel,
         out_shape=[out] * parts,
         grid_spec=pltpu.PrefetchScalarGridSpec(
             num_scalar_prefetch=1,
-            grid=(2 * steps,),
+            grid=(heads // width,),
             in_specs=[
                 pl.BlockSpec((rows, depth), lambda i, h: (0, 0)),
-                pl.BlockSpec(
-                    (planes, width, block),
-                    lambda i, h: (h[lax.div(i, steps)], lax.rem(i, steps), 0),
-                ),
+                pl.BlockSpec((planes, width, block), lambda i, h: (h[0], i, 0)),
             ],
             out_specs=[out_spec] * parts,
         ),
         cost_estimate=pl.CostEstimate(
-            flops=4 * rows * depth * heads,
-            bytes_accessed=2 * (rows * depth + 2 * heads * depth + 2 * rows * heads),
+            flops=2 * rows * depth * heads,
+            bytes_accessed=2 * (rows * depth + heads * depth + rows * heads),
             transcendentals=0,
         ),
-        name="quarter_product",
-    )(halves, g, w)
+        name="half_product",
+    )(half.reshape(1), g, w)
 
 
 def on_device(
@@ -117,9 +114,15 @@
     masked = jnp.where(live, output_gradient, jnp.zeros_like(output_gradient))
 
     quarter = width // ny
-    domain = lax.dynamic_index_in_dim(series_domain, y * nzl + zl, 0, keepdims=False)
-    up = jnp.concatenate([picked(domain_up_map, domain), common_up_map])
-    down = jnp.concatenate([picked(domain_down_map, domain), common_down_map])
+    kinds = lax.iota(jnp.int32, domains)
+    mine = lax.iota(jnp.int32, series_domain.shape[0]) == y * nzl + zl
+    mine = ((series_domain[None, :] == kinds[:, None]) & mine[None, :]).any(1)
+
+    def own_map(maps):
+        return jnp.where(mine[:, None, None], maps, jnp.zeros_like(maps)).sum(0)
+
+    up = jnp.concatenate([own_map(domain_up_map), common_up_map])
+    down = jnp.concatenate([own_map(domain_down_map), common_down_map])
     first = zh == 0
 
     def here(x):
@@ -154,7 +157,7 @@
     far = across(jnp.concatenate([back_own, down], axis=1))
     up_grad = adapter_scale * dot(low_own, cols, NN)
     other = shifted(g, "c", 1)
-    far, other, up_grad = lax.optimization_barrier((far, other, up_grad))
+    far, up_grad = lax.optimization_barrier((far, up_grad))
     back_far, far_down = far[:, :half_rows], far[:, half_rows:]
     back_all = jnp.concatenate(ordered_by(first, back_own, back_far), axis=1)
     down_grad = adapter_scale * dot(back_all, attention_output, NN)
@@ -191,23 +194,24 @@
     packed = jnp.pad(jnp.stack(blocks).reshape(2, lines, piece), ((0, 0), (0, spare), (0, 0)))
     lines = lines + spare
     packed = packed.reshape(2 * nzl, lines // nzl, piece)
-    packed = exchange(packed, ("zh", "zl")).sum(0)
-    packed = to_all(packed, "zl").reshape(lines, piece)
+    packed = exchange(packed.astype(bf16), ("zh", "zl")).astype(f32).sum(0)
+    packed = to_all(packed.astype(bf16), "zl").reshape(lines, piece)
     packed = to_all(packed, "y")
-    packed = jnp.concatenate([packed[i] for i in range(ny)], axis=1)
+    packed = jnp.concatenate([packed[i] for i in range(ny)], axis=1).astype(f32)
     grads = packed[: 2 * (dom + shared)].reshape(2, dom + shared, heads)
     domain_down_gradient, domain_up_gradient = grads[:, :dom].reshape(2, domains, rank, heads)
     common_down_gradient, common_up_gradient = grads[:, dom:]
 
-    parts = quarter_product(g, planes, jnp.stack([1 - zh, zh]), 256, ny)
-    parts = [shifted(parts[k], "y", -k) if k else parts[k] for k in range(ny)]
-
-    def finished(at, maps):
-        part = sum(p[:, at : at + heads].astype(f32) for p in parts)
+    def finished(half, maps):
+        parts = list(half_product(g, planes, half, 256, ny))
+        for k in range(1, ny):
+            parts[k] = shifted(parts[k], "y", -k)
+        part = sum(p.astype(f32) for p in parts)
         return (part + adapter_scale * dot(back_own, maps, TN)).astype(bf16)
 
-    far_out = across(finished(0, far_down))
-    own_out = finished(heads, down)
+    far_out = finished(1 - zh, far_down)
+    far_out = across(far_out)
+    own_out = finished(zh, down)
     grad_input = jnp.concatenate(ordered_by(first, own_out, far_out))
     return (
         grad_input,

time: 232 us -> 220 us (0.948)
  the two profiles are of different devices: /device:TPU:78 before, /device:TPU:32 now
where the time goes in v1:
time: 220 us; the launch traced here: 218 us
  starting transfers between devices  84.7 us (38%)
  waiting for transfers between devices  55.2 us (25%)
  blocking collectives  32 us (15%)
  between operations  15.3 us (7%)
  Pallas kernels  12 us (5%)
  other arithmetic  9.03 us (4%)
  local copies, waits for them, and re-layouts  7.11 us (3%)
  matrix products  3.13 us (1%)
    ppermute x13, starting transfers between devices, shifted(): return lax.ppermute(x, axis, [(i, (i + step) % n) for i in range(n)])  43.1 us
    all_to_all x2, blocking collectives, exchange(): return lax.all_to_all(blocks, axis, 0, 0, tiled=True)  32 us
    ppermute x3, waiting for transfers between devices, across(): return lax.ppermute(x, 'zh', [(0, 1), (1, 0)])  30.9 us
    ppermute x3, starting transfers between devices, across(): return lax.ppermute(x, 'zh', [(0, 1), (1, 0)])  26.6 us
    all_to_all x4, starting transfers between devices, exchange(): return lax.all_to_all(blocks, axis, 0, 0, tiled=True)  15 us
    ppermute x13, waiting for transfers between devices, shifted(): return lax.ppermute(x, axis, [(i, (i + step) % n) for i in range(n)])  12.8 us
    pallas_call x2, Pallas kernels, half_product(): pl.pallas_call(matmul_kernel, out_shape=[out] * parts, grid_spec=pltpu.Pr...  12 us
    all_to_all x4, waiting for transfers between devices, exchange(): return lax.all_to_all(blocks, axis, 0, 0, tiled=True)  11.5 us
  transfers between devices with their start and end apart: 21, of which 8 were waited for; matrix products, arithmetic and copies ran while one was open for 6% of the time, Pallas kernels for 3%

profile of v1, /device:TPU:32, one launch (start us, length us, event | category | flops | bytes accessed | tf_op | source)
XLA Modules:
  0.0 218.5 jit_solution(8072474495542829960)
XLA Ops:
  7.3 0.8 fusion.19
  8.1 1.1 select_reduce_fusion.1
  9.2 0.9 fusion.15
  10.2 0.8 pad_maximum_fusion.10
  11.0 14.8 %collective-permute-start.7 = (bf16[48,896]{1,0:T(8,128)(2,1)S(1)}, bf16[48,896]{1,0:T(8,128)(2,1)S(1)}, u32[]{:S(2)}, u32[]{:S(2)}) collective-permute-start(bf16[48,896]{1,0:T(8,128)(2,1)S(1)} %pad_maximum_fusion.10), channel_id=1, source_target_pairs={{0,8},{8,0},{1,9},{9,1},{2,10},{10,2},{3,11},{11,3},{4,12},{12,4},... | collective-permute-start | bytes 258056 | tf_op jit(solution)/shard_map/ppermute | solution.py:52
  26.7 4.9 %collective-permute-start.2 = (bf16[24,2048]{1,0:T(8,128)(2,1)S(1)}, bf16[24,2048]{1,0:T(8,128)(2,1)S(1)}, u32[]{:S(2)}, u32[]{:S(2)}) collective-permute-start(bf16[24,2048]{1,0:T(8,128)(2,1)S(1)} %get-tuple-element.42), channel_id=1, source_target_pairs={{0,384},{128,0},{256,128},{384,256},{1,385},{129,1},{257,129},{385... | collective-permute-start | bytes 294920 | tf_op jit(solution)/shard_map/ppermute | solution.py:36
  31.7 2.5 %collective-permute-start.1 = (bf16[24,2048]{1,0:T(8,128)(2,1)S(1)}, bf16[24,2048]{1,0:T(8,128)(2,1)S(1)}, u32[]{:S(2)}, u32[]{:S(2)}) collective-permute-start(bf16[24,2048]{1,0:T(8,128)(2,1)S(1)} %get-tuple-element.43), channel_id=1, source_target_pairs={{0,256},{128,384},{256,0},{384,128},{1,257},{129,385},{257,1},{385... | collective-permute-start | bytes 294920 | tf_op jit(solution)/shard_map/ppermute | solution.py:36
  34.2 2.9 %collective-permute-start = (bf16[24,2048]{1,0:T(8,128)(2,1)S(1)}, bf16[24,2048]{1,0:T(8,128)(2,1)S(1)}, u32[]{:S(2)}, u32[]{:S(2)}) collective-permute-start(bf16[24,2048]{1,0:T(8,128)(2,1)S(1)} %get-tuple-element.44), channel_id=1, source_target_pairs={{0,128},{128,256},{256,384},{384,0},{1,129},{129,257},{257,385},{3... | collective-permute-start | bytes 294920 | tf_op jit(solution)/shard_map/ppermute | solution.py:36
  37.3 0.3 copy.22
  37.6 1.0 reshape.102
  38.6 4.3 %all-to-all-start = ((bf16[8,24,1024]{2,1,0:T(8,128)(2,1)}), bf16[8,24,1024]{2,1,0:T(8,128)(2,1)S(1)}, u32[]{:S(2)}, u32[]{:S(2)}) async-start(bf16[8,24,1024]{2,1,0:T(8,128)(2,1)} %reshape.102), calls=%async_computation | async-start | bytes 786432 | tf_op jit(solution)/shard_map/all_to_all | solution.py:26
  43.1 5.1 %collective-permute-start.5 = (bf16[96,2048]{1,0:T(8,128)(2,1)S(1)}, bf16[96,2048]{1,0:T(8,128)(2,1)S(1)}, u32[]{:S(2)}, u32[]{:S(2)}) collective-permute-start(bf16[96,2048]{1,0:T(8,128)(2,1)S(1)} %bitcast.72), channel_id=1, source_target_pairs={{0,6},{2,0},{4,2},{6,4},{1,7},{3,1},{5,3},{7,5},{8,14},{10,8},{12,... | collective-permute-start | bytes 1179656 | tf_op jit(solution)/shard_map/ppermute | solution.py:36
  48.3 2.8 %collective-permute-start.4 = (bf16[96,2048]{1,0:T(8,128)(2,1)S(1)}, bf16[96,2048]{1,0:T(8,128)(2,1)S(1)}, u32[]{:S(2)}, u32[]{:S(2)}) collective-permute-start(bf16[96,2048]{1,0:T(8,128)(2,1)S(1)} %bitcast.73), channel_id=1, source_target_pairs={{0,4},{2,6},{4,0},{6,2},{1,5},{3,7},{5,1},{7,3},{8,12},{10,14},{12... | collective-permute-start | bytes 1179656 | tf_op jit(solution)/shard_map/ppermute | solution.py:36
  51.1 2.8 %collective-permute-start.3 = (bf16[96,2048]{1,0:T(8,128)(2,1)S(1)}, bf16[96,2048]{1,0:T(8,128)(2,1)S(1)}, u32[]{:S(2)}, u32[]{:S(2)}) collective-permute-start(bf16[96,2048]{1,0:T(8,128)(2,1)S(1)} %bitcast.74), channel_id=1, source_target_pairs={{0,2},{2,4},{4,6},{6,0},{1,3},{3,5},{5,7},{7,1},{8,10},{10,12},{12... | collective-permute-start | bytes 1179656 | tf_op jit(solution)/shard_map/ppermute | solution.py:36
  54.2 0.9 broadcast_in_dim.32
  55.1 3.7 %all-to-all-start.1 = ((f32[8,48,384]{2,1,0:T(8,128)}), f32[8,48,384]{2,1,0:T(8,128)S(1)}, u32[]{:S(2)}, u32[]{:S(2)}) async-start(f32[8,48,384]{2,1,0:T(8,128)} %broadcast_in_dim.32), calls=%async_computation.1 | async-start | bytes 1179648 | tf_op jit(solution)/shard_map/all_to_all | solution.py:26
  59.3 4.4 %collective-permute-done.4 = bf16[96,2048]{1,0:T(8,128)(2,1)S(1)} collective-permute-done((bf16[96,2048]{1,0:T(8,128)(2,1)S(1)}, bf16[96,2048]{1,0:T(8,128)(2,1)S(1)}, u32[]{:S(2)}, u32[]{:S(2)}) %collective-permute-start.4) | collective-permute-done | bytes 393248 | tf_op jit(solution)/shard_map/ppermute | solution.py:36
  63.7 8.1 %collective-permute-done.3 = bf16[96,2048]{1,0:T(8,128)(2,1)S(1)} collective-permute-done((bf16[96,2048]{1,0:T(8,128)(2,1)S(1)}, bf16[96,2048]{1,0:T(8,128)(2,1)S(1)}, u32[]{:S(2)}, u32[]{:S(2)}) %collective-permute-start.3) | collective-permute-done | bytes 393248 | tf_op jit(solution)/shard_map/ppermute | solution.py:36
  71.9 1.4 pad_maximum_fusion.1
  73.2 1.9 collective-permute-start.6
  75.1 2.2 all-to-all-done.1
  77.5 1.9 collective-permute-start.8
  79.7 17.9 %collective-permute-done.8 = bf16[48,704]{1,0:T(8,128)(2,1)S(1)} collective-permute-done((bf16[48,704]{1,0:T(8,128)(2,1)S(1)}, bf16[48,704]{1,0:T(8,128)(2,1)S(1)}, u32[]{:S(2)}, u32[]{:S(2)}) %collective-permute-start.8) | collective-permute-done | bytes 67616 | tf_op jit(solution)/shard_map/ppermute | solution.py:52
  97.9 0.7 pad_maximum_fusion.8
  98.7 3.6 %all-to-all-start.2 = ((f32[4,144,128]{2,1,0:T(8,128)}), f32[4,144,128]{2,1,0:T(8,128)S(1)}, u32[]{:S(2)}, u32[]{:S(2)}) async-start(f32[4,144,128]{2,1,0:T(8,128)} %pad_maximum_fusion.8), calls=%async_computation.2 | async-start | bytes 589824 | tf_op jit(solution)/shard_map/all_to_all | solution.py:26
  102.2 1.7 select_bitcast_fusion
  104.2 0.4 pad_maximum_fusion
  104.7 2.1 copy.18
  106.8 2.3 %all-to-all-done.2 = f32[4,144,128]{2,1,0:T(8,128)S(1)} async-done(((f32[4,144,128]{2,1,0:T(8,128)}), f32[4,144,128]{2,1,0:T(8,128)S(1)}, u32[]{:S(2)}, u32[]{:S(2)}) %all-to-all-start.2) | async-done | bytes 294944 | tf_op jit(solution)/shard_map/all_to_all | solution.py:26
  109.3 17.8 %all_to_all.30 = bf16[16,40,128]{2,1,0:T(8,128)(2,1)S(1)} all-to-all(bf16[16,40,128]{2,1,0:T(8,128)(2,1)S(1)} %bitcast.92), channel_id=1, replica_groups=mesh['y'=4,'zl'=8,'zh'=2,'x'=4,'c'=2] {'zh','zl'}, dimensions={0} | all-to-all | bytes 327680 | tf_op jit(solution)/shard_map/all_to_all | solution.py:26
  127.2 14.1 %all_to_all.31 = bf16[8,40,128]{2,1,0:T(8,128)(2,1)S(1)} all-to-all(bf16[8,40,128]{2,1,0:T(8,128)(2,1)S(1)} %broadcast_in_dim.54), channel_id=1, replica_groups=mesh['y'=4,'zl'=8,'zh'=2,'x'=4,'c'=2] {'zl'}, dimensions={0} | all-to-all | bytes 163840 | tf_op jit(solution)/shard_map/all_to_all | solution.py:26
  141.4 0.8 broadcast_in_dim.56
  142.1 3.5 %all-to-all-start.5 = ((bf16[4,320,128]{2,1,0:T(8,128)(2,1)}), bf16[4,320,128]{2,1,0:T(8,128)(2,1)S(1)}, u32[]{:S(2)}, u32[]{:S(2)}) async-start(bf16[4,320,128]{2,1,0:T(8,128)(2,1)} %broadcast_in_dim.56), calls=%async_computation.5 | async-start | bytes 655360 | tf_op jit(solution)/shard_map/all_to_all | solution.py:26
  145.6 7.0 %all-to-all-done.5 = bf16[4,320,128]{2,1,0:T(8,128)(2,1)S(1)} async-done(((bf16[4,320,128]{2,1,0:T(8,128)(2,1)}), bf16[4,320,128]{2,1,0:T(8,128)(2,1)S(1)}, u32[]{:S(2)}, u32[]{:S(2)}) %all-to-all-start.5) | async-done | bytes 327712 | tf_op jit(solution)/shard_map/all_to_all | solution.py:26
  152.7 6.0 %half_product.3 = (bf16[192,512]{1,0:T(8,128)(2,1)}, bf16[192,512]{1,0:T(8,128)(2,1)}, bf16[192,512]{1,0:T(8,128)(2,1)}, bf16[192,512]{1,0:T(8,128)(2,1)}) custom-call(s32[1]{0:T(128)} %bitcast.24.half, bf16[768,2048]{1,0:T(8,128)(2,1)} %bitcast.65, bf16[16,512,256]{2,1,0:T(8,128)(2,1)} %bitcast.67), custom_call_target="tpu_custom_call" | custom-call | flops 1610612736 | bytes 6029312 | tf_op jit(solution)/shard_map/half_product/pallas_call | solution.py:68
  158.7 2.5 %collective-permute-start.14 = (bf16[192,512]{1,0:T(8,128)(2,1)}, bf16[192,512]{1,0:T(8,128)(2,1)S(1)}, u32[]{:S(2)}, u32[]{:S(2)}) collective-permute-start(bf16[192,512]{1,0:T(8,128)(2,1)} %get-tuple-element.27), channel_id=1, source_target_pairs={{0,128},{128,256},{256,384},{384,0},{1,129},{129,257},{257,385},{3... | collective-permute-start | bytes 589832 | tf_op jit(solution)/shard_map/ppermute | solution.py:36
  161.2 4.0 %collective-permute-start.13 = (bf16[192,512]{1,0:T(8,128)(2,1)}, bf16[192,512]{1,0:T(8,128)(2,1)S(1)}, u32[]{:S(2)}, u32[]{:S(2)}) collective-permute-start(bf16[192,512]{1,0:T(8,128)(2,1)} %get-tuple-element.26), channel_id=1, source_target_pairs={{0,256},{128,384},{256,0},{384,128},{1,257},{129,385},{257,1},{385... | collective-permute-start | bytes 589832 | tf_op jit(solution)/shard_map/ppermute | solution.py:36
  165.2 2.5 %collective-permute-start.12 = (bf16[192,512]{1,0:T(8,128)(2,1)}, bf16[192,512]{1,0:T(8,128)(2,1)S(1)}, u32[]{:S(2)}, u32[]{:S(2)}) collective-permute-start(bf16[192,512]{1,0:T(8,128)(2,1)} %get-tuple-element.25), channel_id=1, source_target_pairs={{0,384},{128,0},{256,128},{384,256},{1,385},{129,1},{257,129},{385... | collective-permute-start | bytes 589832 | tf_op jit(solution)/shard_map/ppermute | solution.py:36
  167.7 0.9 fusion.27
  168.6 6.0 %half_product.2 = (bf16[192,512]{1,0:T(8,128)(2,1)}, bf16[192,512]{1,0:T(8,128)(2,1)}, bf16[192,512]{1,0:T(8,128)(2,1)}, bf16[192,512]{1,0:T(8,128)(2,1)}) custom-call(s32[1]{0:T(128)} %bitcast.half, bf16[768,2048]{1,0:T(8,128)(2,1)} %bitcast.66, bf16[16,512,256]{2,1,0:T(8,128)(2,1)} %bitcast.68), custom_call_target="tpu_custom_call" | custom-call | flops 1610612736 | bytes 6029312 | tf_op jit(solution)/shard_map/half_product/pallas_call | solution.py:68
  174.6 3.3 %collective-permute-start.11 = (bf16[192,512]{1,0:T(8,128)(2,1)}, bf16[192,512]{1,0:T(8,128)(2,1)S(1)}, u32[]{:S(2)}, u32[]{:S(2)}) collective-permute-start(bf16[192,512]{1,0:T(8,128)(2,1)} %get-tuple-element.23), channel_id=1, source_target_pairs={{0,128},{128,256},{256,384},{384,0},{1,129},{129,257},{257,385},{3... | collective-permute-start | bytes 589832 | tf_op jit(solution)/shard_map/ppermute | solution.py:36
  177.9 3.4 %collective-permute-start.10 = (bf16[192,512]{1,0:T(8,128)(2,1)}, bf16[192,512]{1,0:T(8,128)(2,1)S(1)}, u32[]{:S(2)}, u32[]{:S(2)}) collective-permute-start(bf16[192,512]{1,0:T(8,128)(2,1)} %get-tuple-element.22), channel_id=1, source_target_pairs={{0,256},{128,384},{256,0},{384,128},{1,257},{129,385},{257,1},{385... | collective-permute-start | bytes 589832 | tf_op jit(solution)/shard_map/ppermute | solution.py:36
  181.4 4.5 %collective-permute-start.9 = (bf16[192,512]{1,0:T(8,128)(2,1)}, bf16[192,512]{1,0:T(8,128)(2,1)S(1)}, u32[]{:S(2)}, u32[]{:S(2)}) collective-permute-start(bf16[192,512]{1,0:T(8,128)(2,1)} %get-tuple-element.21), channel_id=1, source_target_pairs={{0,384},{128,0},{256,128},{384,256},{1,385},{129,1},{257,129},{385... | collective-permute-start | bytes 589832 | tf_op jit(solution)/shard_map/ppermute | solution.py:36
  186.2 9.9 %collective-permute-start.15 = (bf16[192,512]{1,0:T(8,128)(2,1)S(1)}, bf16[192,512]{1,0:T(8,128)(2,1)S(1)}, u32[]{:S(2)}, u32[]{:S(2)}) collective-permute-start(bf16[192,512]{1,0:T(8,128)(2,1)S(1)} %add_convert_fusion), channel_id=1, source_target_pairs={{0,8},{8,0},{1,9},{9,1},{2,10},{10,2},{3,11},{11,3},{4,12},{12,4},... | collective-permute-start | bytes 589832 | tf_op jit(solution)/shard_map/ppermute | solution.py:52
  196.1 0.6 slice_bitcast_fusion.4
  196.7 12.9 %collective-permute-done.15 = bf16[192,512]{1,0:T(8,128)(2,1)S(1)} collective-permute-done((bf16[192,512]{1,0:T(8,128)(2,1)S(1)}, bf16[192,512]{1,0:T(8,128)(2,1)S(1)}, u32[]{:S(2)}, u32[]{:S(2)}) %collective-permute-start.15) | collective-permute-done | bytes 196640 | tf_op jit(solution)/shard_map/ppermute | solution.py:52
  209.7 1.2 broadcast_select_fusion.2
  210.9 0.8 pad_maximum_fusion.3
  (68 shorter events, 3.2 us)
Async XLA Ops:
  7.2 2.0 copy-start
  7.2 19.4 %copy-start.1 = (bf16[24,8192]{1,0:T(8,128)(2,1)S(1)}, bf16[24,8192]{1,0:T(8,128)(2,1)}, u32[]{:S(2)}) copy-start(bf16[24,8192]{1,0:T(8,128)(2,1)} %param.9) | copy-start | bytes 1179652
  7.2 145.5 %all-gather.3.cloned.1.call-start = ((), (), s32[]{:S(2)}) async-start(), calls=%async_computation.6 | async-start | bytes 4456448 | tf_op jit(solution)/shard_map/all_gather | solution.py:110
  11.0 31.8 %collective-permute-start.7 = (bf16[48,896]{1,0:T(8,128)(2,1)S(1)}, bf16[48,896]{1,0:T(8,128)(2,1)S(1)}, u32[]{:S(2)}, u32[]{:S(2)}) collective-permute-start(bf16[48,896]{1,0:T(8,128)(2,1)S(1)} %pad_maximum_fusion.10), channel_id=1, source_target_pairs={{0,8},{8,0},{1,9},{9,1},{2,10},{10,2},{3,11},{11,3},{4,12},{12,4},... | collective-permute-start | bytes 258056 | tf_op jit(solution)/shard_map/ppermute | solution.py:52
  26.7 16.3 %collective-permute-start.2 = (bf16[24,2048]{1,0:T(8,128)(2,1)S(1)}, bf16[24,2048]{1,0:T(8,128)(2,1)S(1)}, u32[]{:S(2)}, u32[]{:S(2)}) collective-permute-start(bf16[24,2048]{1,0:T(8,128)(2,1)S(1)} %get-tuple-element.42), channel_id=1, source_target_pairs={{0,384},{128,0},{256,128},{384,256},{1,385},{129,1},{257,129},{385... | collective-permute-start | bytes 294920 | tf_op jit(solution)/shard_map/ppermute | solution.py:36
  31.7 11.4 %collective-permute-start.1 = (bf16[24,2048]{1,0:T(8,128)(2,1)S(1)}, bf16[24,2048]{1,0:T(8,128)(2,1)S(1)}, u32[]{:S(2)}, u32[]{:S(2)}) collective-permute-start(bf16[24,2048]{1,0:T(8,128)(2,1)S(1)} %get-tuple-element.43), channel_id=1, source_target_pairs={{0,256},{128,384},{256,0},{384,128},{1,257},{129,385},{257,1},{385... | collective-permute-start | bytes 294920 | tf_op jit(solution)/shard_map/ppermute | solution.py:36
  34.2 8.8 %collective-permute-start = (bf16[24,2048]{1,0:T(8,128)(2,1)S(1)}, bf16[24,2048]{1,0:T(8,128)(2,1)S(1)}, u32[]{:S(2)}, u32[]{:S(2)}) collective-permute-start(bf16[24,2048]{1,0:T(8,128)(2,1)S(1)} %get-tuple-element.44), channel_id=1, source_target_pairs={{0,128},{128,256},{256,384},{384,0},{1,129},{129,257},{257,385},{3... | collective-permute-start | bytes 294920 | tf_op jit(solution)/shard_map/ppermute | solution.py:36
  37.1 5.9 %copy-start.3 = (bf16[16,512]{1,0:T(8,128)(2,1)S(1)}, bf16[16,512]{1,0:T(8,128)(2,1)}, u32[]{:S(2)}) copy-start(bf16[16,512]{1,0:T(8,128)(2,1)} %param.15) | copy-start | bytes 49156
  38.6 15.3 %all-to-all-start = ((bf16[8,24,1024]{2,1,0:T(8,128)(2,1)}), bf16[8,24,1024]{2,1,0:T(8,128)(2,1)S(1)}, u32[]{:S(2)}, u32[]{:S(2)}) async-start(bf16[8,24,1024]{2,1,0:T(8,128)(2,1)} %reshape.102), calls=%async_computation | async-start | bytes 786432 | tf_op jit(solution)/shard_map/all_to_all | solution.py:26
  43.1 15.6 %copy-start.5 = (s32[32]{0:T(128)S(1)}, s32[32]{0:T(128)}, u32[]{:S(2)}) copy-start(s32[32]{0:T(128)} %param.17) | copy-start | bytes 388
  43.1 16.1 %collective-permute-start.5 = (bf16[96,2048]{1,0:T(8,128)(2,1)S(1)}, bf16[96,2048]{1,0:T(8,128)(2,1)S(1)}, u32[]{:S(2)}, u32[]{:S(2)}) collective-permute-start(bf16[96,2048]{1,0:T(8,128)(2,1)S(1)} %bitcast.72), channel_id=1, source_target_pairs={{0,6},{2,0},{4,2},{6,4},{1,7},{3,1},{5,3},{7,5},{8,14},{10,8},{12,... | collective-permute-start | bytes 1179656 | tf_op jit(solution)/shard_map/ppermute | solution.py:36
  48.3 15.4 %collective-permute-start.4 = (bf16[96,2048]{1,0:T(8,128)(2,1)S(1)}, bf16[96,2048]{1,0:T(8,128)(2,1)S(1)}, u32[]{:S(2)}, u32[]{:S(2)}) collective-permute-start(bf16[96,2048]{1,0:T(8,128)(2,1)S(1)} %bitcast.73), channel_id=1, source_target_pairs={{0,4},{2,6},{4,0},{6,2},{1,5},{3,7},{5,1},{7,3},{8,12},{10,14},{12... | collective-permute-start | bytes 1179656 | tf_op jit(solution)/shard_map/ppermute | solution.py:36
  51.1 20.8 %collective-permute-start.3 = (bf16[96,2048]{1,0:T(8,128)(2,1)S(1)}, bf16[96,2048]{1,0:T(8,128)(2,1)S(1)}, u32[]{:S(2)}, u32[]{:S(2)}) collective-permute-start(bf16[96,2048]{1,0:T(8,128)(2,1)S(1)} %bitcast.74), channel_id=1, source_target_pairs={{0,2},{2,4},{4,6},{6,0},{1,3},{3,5},{5,7},{7,1},{8,10},{10,12},{12... | collective-permute-start | bytes 1179656 | tf_op jit(solution)/shard_map/ppermute | solution.py:36
  55.1 22.3 %all-to-all-start.1 = ((f32[8,48,384]{2,1,0:T(8,128)}), f32[8,48,384]{2,1,0:T(8,128)S(1)}, u32[]{:S(2)}, u32[]{:S(2)}) async-start(f32[8,48,384]{2,1,0:T(8,128)} %broadcast_in_dim.32), calls=%async_computation.1 | async-start | bytes 1179648 | tf_op jit(solution)/shard_map/all_to_all | solution.py:26
  71.9 5.5 %copy-start.4 = (bf16[16,512]{1,0:T(8,128)(2,1)S(1)}, bf16[16,512]{1,0:T(8,128)(2,1)}, u32[]{:S(2)}) copy-start(bf16[16,512]{1,0:T(8,128)(2,1)} %param.14) | copy-start | bytes 49156
  73.2 29.0 %collective-permute-start.6 = (bf16[4,96,2048]{2,1,0:T(8,128)(2,1)}, bf16[4,96,2048]{2,1,0:T(8,128)(2,1)}, u32[]{:S(2)}, u32[]{:S(2)}) collective-permute-start(bf16[4,96,2048]{2,1,0:T(8,128)(2,1)} %pad_maximum_fusion.1), channel_id=1, source_target_pairs={{0,1},{1,0},{2,3},{3,2},{4,5},{5,4},{6,7},{7,6},{8,9},{9,8},{10,11... | collective-permute-start | bytes 4718600 | tf_op jit(solution)/shard_map/ppermute | solution.py:36
  77.5 20.1 %collective-permute-start.8 = (bf16[48,704]{1,0:T(8,128)(2,1)S(1)}, bf16[48,704]{1,0:T(8,128)(2,1)S(1)}, u32[]{:S(2)}, u32[]{:S(2)}) collective-permute-start(bf16[48,704]{1,0:T(8,128)(2,1)S(1)} %maximum_maximum_fusion), channel_id=1, source_target_pairs={{0,8},{8,0},{1,9},{9,1},{2,10},{10,2},{3,11},{11,3},{4,12},{12,4},... | collective-permute-start | bytes 202760 | tf_op jit(solution)/shard_map/ppermute | solution.py:52
  98.7 10.4 %all-to-all-start.2 = ((f32[4,144,128]{2,1,0:T(8,128)}), f32[4,144,128]{2,1,0:T(8,128)S(1)}, u32[]{:S(2)}, u32[]{:S(2)}) async-start(f32[4,144,128]{2,1,0:T(8,128)} %pad_maximum_fusion.8), calls=%async_computation.2 | async-start | bytes 589824 | tf_op jit(solution)/shard_map/all_to_all | solution.py:26
  142.1 10.5 %all-to-all-start.5 = ((bf16[4,320,128]{2,1,0:T(8,128)(2,1)}), bf16[4,320,128]{2,1,0:T(8,128)(2,1)S(1)}, u32[]{:S(2)}, u32[]{:S(2)}) async-start(bf16[4,320,128]{2,1,0:T(8,128)(2,1)} %broadcast_in_dim.56), calls=%async_computation.5 | async-start | bytes 655360 | tf_op jit(solution)/shard_map/all_to_all | solution.py:26
  158.7 22.7 %collective-permute-start.14 = (bf16[192,512]{1,0:T(8,128)(2,1)}, bf16[192,512]{1,0:T(8,128)(2,1)S(1)}, u32[]{:S(2)}, u32[]{:S(2)}) collective-permute-start(bf16[192,512]{1,0:T(8,128)(2,1)} %get-tuple-element.27), channel_id=1, source_target_pairs={{0,128},{128,256},{256,384},{384,0},{1,129},{129,257},{257,385},{3... | collective-permute-start | bytes 589832 | tf_op jit(solution)/shard_map/ppermute | solution.py:36
  161.2 24.7 %collective-permute-start.13 = (bf16[192,512]{1,0:T(8,128)(2,1)}, bf16[192,512]{1,0:T(8,128)(2,1)S(1)}, u32[]{:S(2)}, u32[]{:S(2)}) collective-permute-start(bf16[192,512]{1,0:T(8,128)(2,1)} %get-tuple-element.26), channel_id=1, source_target_pairs={{0,256},{128,384},{256,0},{384,128},{1,257},{129,385},{257,1},{385... | collective-permute-start | bytes 589832 | tf_op jit(solution)/shard_map/ppermute | solution.py:36
  165.2 20.8 %collective-permute-start.12 = (bf16[192,512]{1,0:T(8,128)(2,1)}, bf16[192,512]{1,0:T(8,128)(2,1)S(1)}, u32[]{:S(2)}, u32[]{:S(2)}) collective-permute-start(bf16[192,512]{1,0:T(8,128)(2,1)} %get-tuple-element.25), channel_id=1, source_target_pairs={{0,384},{128,0},{256,128},{384,256},{1,385},{129,1},{257,129},{385... | collective-permute-start | bytes 589832 | tf_op jit(solution)/shard_map/ppermute | solution.py:36
  168.6 17.3 %copy-start.2 = (bf16[192,512]{1,0:T(8,128)(2,1)S(1)}, bf16[192,512]{1,0:T(8,128)(2,1)}, u32[]{:S(2)}) copy-start(bf16[192,512]{1,0:T(8,128)(2,1)} %get-tuple-element.24) | copy-start | bytes 589828
  174.6 22.1 %collective-permute-start.11 = (bf16[192,512]{1,0:T(8,128)(2,1)}, bf16[192,512]{1,0:T(8,128)(2,1)S(1)}, u32[]{:S(2)}, u32[]{:S(2)}) collective-permute-start(bf16[192,512]{1,0:T(8,128)(2,1)} %get-tuple-element.23), channel_id=1, source_target_pairs={{0,128},{128,256},{256,384},{384,0},{1,129},{129,257},{257,385},{3... | collective-permute-start | bytes 589832 | tf_op jit(solution)/shard_map/ppermute | solution.py:36
  177.9 18.8 %collective-permute-start.10 = (bf16[192,512]{1,0:T(8,128)(2,1)}, bf16[192,512]{1,0:T(8,128)(2,1)S(1)}, u32[]{:S(2)}, u32[]{:S(2)}) collective-permute-start(bf16[192,512]{1,0:T(8,128)(2,1)} %get-tuple-element.22), channel_id=1, source_target_pairs={{0,256},{128,384},{256,0},{384,128},{1,257},{129,385},{257,1},{385... | collective-permute-start | bytes 589832 | tf_op jit(solution)/shard_map/ppermute | solution.py:36
  181.4 15.4 %collective-permute-start.9 = (bf16[192,512]{1,0:T(8,128)(2,1)}, bf16[192,512]{1,0:T(8,128)(2,1)S(1)}, u32[]{:S(2)}, u32[]{:S(2)}) collective-permute-start(bf16[192,512]{1,0:T(8,128)(2,1)} %get-tuple-element.21), channel_id=1, source_target_pairs={{0,384},{128,0},{256,128},{384,256},{1,385},{129,1},{257,129},{385... | collective-permute-start | bytes 589832 | tf_op jit(solution)/shard_map/ppermute | solution.py:36
  186.2 23.4 %collective-permute-start.15 = (bf16[192,512]{1,0:T(8,128)(2,1)S(1)}, bf16[192,512]{1,0:T(8,128)(2,1)S(1)}, u32[]{:S(2)}, u32[]{:S(2)}) collective-permute-start(bf16[192,512]{1,0:T(8,128)(2,1)S(1)} %add_convert_fusion), channel_id=1, source_target_pairs={{0,8},{8,0},{1,9},{9,1},{2,10},{10,2},{3,11},{11,3},{4,12},{12,4},... | collective-permute-start | bytes 589832 | tf_op jit(solution)/shard_map/ppermute | solution.py:52
Sparse Core Ops, SparseCore 0:
  26.0 77.4 all-gather.2

commit v2 on v1

--- a/solution.py
+++ b/solution.py
@@ -115,11 +115,11 @@
 
     quarter = width // ny
     kinds = lax.iota(jnp.int32, domains)
-    mine = lax.iota(jnp.int32, series_domain.shape[0]) == y * nzl + zl
-    mine = ((series_domain[None, :] == kinds[:, None]) & mine[None, :]).any(1)
+    at_own = lax.iota(jnp.int32, series_domain.shape[0]) == y * nzl + zl
+    own_kind = ((series_domain[None, :] == kinds[:, None]) & at_own[None, :]).any(1)
 
     def own_map(maps):
-        return jnp.where(mine[:, None, None], maps, jnp.zeros_like(maps)).sum(0)
+        return jnp.where(own_kind[:, None, None], maps, jnp.zeros_like(maps)).sum(0)
 
     up = jnp.concatenate([own_map(domain_up_map), common_up_map])
     down = jnp.concatenate([own_map(domain_down_map), common_down_map])
@@ -212,7 +212,8 @@
     far_out = finished(1 - zh, far_down)
     far_out = across(far_out)
     own_out = finished(zh, down)
-    grad_input = jnp.concatenate(ordered_by(first, own_out, far_out))
+    mine = (lax.iota(jnp.int32, 2) == zh)[:, None, None]
+    grad_input = jnp.where(mine, own_out[None], far_out[None]).reshape(2 * half_rows, heads)
     return (
         grad_input,
         domain_down_gradient,

time: 220 us -> 219 us (level)
  transfers between devices with their start and end apart: 21 -> 21, of which waited for: 8 -> 8; matrix products, arithmetic and copies ran while one was open for 6% -> 7% of each run, Pallas kernels for 3% -> 3%
where the time goes in v2:
time: 219 us; the launch traced here: 218 us
  starting transfers between devices  86.2 us (39%)
  waiting for transfers between devices  53.3 us (24%)
  blocking collectives  32 us (15%)
  between operations  15.3 us (7%)
  Pallas kernels  11.9 us (5%)
  other arithmetic  9.14 us (4%)
  local copies, waits for them, and re-layouts  7.25 us (3%)
  matrix products  3.07 us (1%)
    ppermute x13, starting transfers between devices, shifted(): return lax.ppermute(x, axis, [(i, (i + step) % n) for i in range(n)])  43.1 us
    all_to_all x2, blocking collectives, exchange(): return lax.all_to_all(blocks, axis, 0, 0, tiled=True)  32 us
    ppermute x3, waiting for transfers between devices, across(): return lax.ppermute(x, 'zh', [(0, 1), (1, 0)])  29.2 us
    ppermute x3, starting transfers between devices, across(): return lax.ppermute(x, 'zh', [(0, 1), (1, 0)])  26.6 us
    all_to_all x4, starting transfers between devices, exchange(): return lax.all_to_all(blocks, axis, 0, 0, tiled=True)  16.5 us
    ppermute x13, waiting for transfers between devices, shifted(): return lax.ppermute(x, axis, [(i, (i + step) % n) for i in range(n)])  12.8 us
    pallas_call x2, Pallas kernels, half_product(): pl.pallas_call(matmul_kernel, out_shape=[out] * parts, grid_spec=pltpu.Pr...  11.9 us
    all_to_all x4, waiting for transfers between devices, exchange(): return lax.all_to_all(blocks, axis, 0, 0, tiled=True)  11.3 us
  transfers between devices with their start and end apart: 21, of which 8 were waited for; matrix products, arithmetic and copies ran while one was open for 7% of the time, Pallas kernels for 3%

profile of v2, /device:TPU:32, one launch (start us, length us, event | category | flops | bytes accessed | tf_op | source)
XLA Modules:
  0.0 218.3 jit_solution(3829017039319357850)
XLA Ops:
  7.3 0.8 fusion.19
  8.1 1.1 select_reduce_fusion.1
  9.2 0.9 fusion.15
  10.2 0.8 pad_maximum_fusion.9
  11.0 14.8 %collective-permute-start.7 = (bf16[48,896]{1,0:T(8,128)(2,1)S(1)}, bf16[48,896]{1,0:T(8,128)(2,1)S(1)}, u32[]{:S(2)}, u32[]{:S(2)}) collective-permute-start(bf16[48,896]{1,0:T(8,128)(2,1)S(1)} %pad_maximum_fusion.9), channel_id=1, source_target_pairs={{0,8},{8,0},{1,9},{9,1},{2,10},{10,2},{3,11},{11,3},{4,12},{12,4},... | collective-permute-start | bytes 258056 | tf_op jit(solution)/shard_map/ppermute | solution.py:52
  26.7 4.9 %collective-permute-start.2 = (bf16[24,2048]{1,0:T(8,128)(2,1)S(1)}, bf16[24,2048]{1,0:T(8,128)(2,1)S(1)}, u32[]{:S(2)}, u32[]{:S(2)}) collective-permute-start(bf16[24,2048]{1,0:T(8,128)(2,1)S(1)} %get-tuple-element.40), channel_id=1, source_target_pairs={{0,384},{128,0},{256,128},{384,256},{1,385},{129,1},{257,129},{385... | collective-permute-start | bytes 294920 | tf_op jit(solution)/shard_map/ppermute | solution.py:36
  31.7 2.5 %collective-permute-start.1 = (bf16[24,2048]{1,0:T(8,128)(2,1)S(1)}, bf16[24,2048]{1,0:T(8,128)(2,1)S(1)}, u32[]{:S(2)}, u32[]{:S(2)}) collective-permute-start(bf16[24,2048]{1,0:T(8,128)(2,1)S(1)} %get-tuple-element.41), channel_id=1, source_target_pairs={{0,256},{128,384},{256,0},{384,128},{1,257},{129,385},{257,1},{385... | collective-permute-start | bytes 294920 | tf_op jit(solution)/shard_map/ppermute | solution.py:36
  34.2 2.9 %collective-permute-start = (bf16[24,2048]{1,0:T(8,128)(2,1)S(1)}, bf16[24,2048]{1,0:T(8,128)(2,1)S(1)}, u32[]{:S(2)}, u32[]{:S(2)}) collective-permute-start(bf16[24,2048]{1,0:T(8,128)(2,1)S(1)} %get-tuple-element.42), channel_id=1, source_target_pairs={{0,128},{128,256},{256,384},{384,0},{1,129},{129,257},{257,385},{3... | collective-permute-start | bytes 294920 | tf_op jit(solution)/shard_map/ppermute | solution.py:36
  37.3 0.3 copy.22
  37.6 1.0 reshape.112
  38.6 4.3 %all-to-all-start = ((bf16[8,24,1024]{2,1,0:T(8,128)(2,1)}), bf16[8,24,1024]{2,1,0:T(8,128)(2,1)S(1)}, u32[]{:S(2)}, u32[]{:S(2)}) async-start(bf16[8,24,1024]{2,1,0:T(8,128)(2,1)} %reshape.112), calls=%async_computation | async-start | bytes 786432 | tf_op jit(solution)/shard_map/all_to_all | solution.py:26
  43.1 5.1 %collective-permute-start.5 = (bf16[96,2048]{1,0:T(8,128)(2,1)S(1)}, bf16[96,2048]{1,0:T(8,128)(2,1)S(1)}, u32[]{:S(2)}, u32[]{:S(2)}) collective-permute-start(bf16[96,2048]{1,0:T(8,128)(2,1)S(1)} %bitcast.76), channel_id=1, source_target_pairs={{0,6},{2,0},{4,2},{6,4},{1,7},{3,1},{5,3},{7,5},{8,14},{10,8},{12,... | collective-permute-start | bytes 1179656 | tf_op jit(solution)/shard_map/ppermute | solution.py:36
  48.3 2.8 %collective-permute-start.4 = (bf16[96,2048]{1,0:T(8,128)(2,1)S(1)}, bf16[96,2048]{1,0:T(8,128)(2,1)S(1)}, u32[]{:S(2)}, u32[]{:S(2)}) collective-permute-start(bf16[96,2048]{1,0:T(8,128)(2,1)S(1)} %bitcast.77), channel_id=1, source_target_pairs={{0,4},{2,6},{4,0},{6,2},{1,5},{3,7},{5,1},{7,3},{8,12},{10,14},{12... | collective-permute-start | bytes 1179656 | tf_op jit(solution)/shard_map/ppermute | solution.py:36
  51.1 2.8 %collective-permute-start.3 = (bf16[96,2048]{1,0:T(8,128)(2,1)S(1)}, bf16[96,2048]{1,0:T(8,128)(2,1)S(1)}, u32[]{:S(2)}, u32[]{:S(2)}) collective-permute-start(bf16[96,2048]{1,0:T(8,128)(2,1)S(1)} %bitcast.78), channel_id=1, source_target_pairs={{0,2},{2,4},{4,6},{6,0},{1,3},{3,5},{5,7},{7,1},{8,10},{10,12},{12... | collective-permute-start | bytes 1179656 | tf_op jit(solution)/shard_map/ppermute | solution.py:36
  54.2 0.9 broadcast_in_dim.91
  55.0 3.7 %all-to-all-start.1 = ((f32[8,48,384]{2,1,0:T(8,128)}), f32[8,48,384]{2,1,0:T(8,128)S(1)}, u32[]{:S(2)}, u32[]{:S(2)}) async-start(f32[8,48,384]{2,1,0:T(8,128)} %broadcast_in_dim.91), calls=%async_computation.1 | async-start | bytes 1179648 | tf_op jit(solution)/shard_map/all_to_all | solution.py:26
  59.3 4.4 %collective-permute-done.4 = bf16[96,2048]{1,0:T(8,128)(2,1)S(1)} collective-permute-done((bf16[96,2048]{1,0:T(8,128)(2,1)S(1)}, bf16[96,2048]{1,0:T(8,128)(2,1)S(1)}, u32[]{:S(2)}, u32[]{:S(2)}) %collective-permute-start.4) | collective-permute-done | bytes 393248 | tf_op jit(solution)/shard_map/ppermute | solution.py:36
  63.7 8.1 %collective-permute-done.3 = bf16[96,2048]{1,0:T(8,128)(2,1)S(1)} collective-permute-done((bf16[96,2048]{1,0:T(8,128)(2,1)S(1)}, bf16[96,2048]{1,0:T(8,128)(2,1)S(1)}, u32[]{:S(2)}, u32[]{:S(2)}) %collective-permute-start.3) | collective-permute-done | bytes 393248 | tf_op jit(solution)/shard_map/ppermute | solution.py:36
  71.9 1.4 pad_maximum_fusion.1
  73.2 1.9 collective-permute-start.6
  75.2 2.2 all-to-all-done.1
  77.5 1.9 collective-permute-start.8
  79.7 16.5 %collective-permute-done.8 = bf16[48,704]{1,0:T(8,128)(2,1)S(1)} collective-permute-done((bf16[48,704]{1,0:T(8,128)(2,1)S(1)}, bf16[48,704]{1,0:T(8,128)(2,1)S(1)}, u32[]{:S(2)}, u32[]{:S(2)}) %collective-permute-start.8) | collective-permute-done | bytes 67616 | tf_op jit(solution)/shard_map/ppermute | solution.py:52
  96.5 0.7 pad_maximum_fusion.7
  97.2 5.1 %all-to-all-start.2 = ((f32[4,144,128]{2,1,0:T(8,128)}), f32[4,144,128]{2,1,0:T(8,128)S(1)}, u32[]{:S(2)}, u32[]{:S(2)}) async-start(f32[4,144,128]{2,1,0:T(8,128)} %pad_maximum_fusion.7), calls=%async_computation.2 | async-start | bytes 589824 | tf_op jit(solution)/shard_map/all_to_all | solution.py:26
  102.3 1.7 select_bitcast_fusion
  104.3 0.4 pad_maximum_fusion
  104.7 2.1 copy.18
  106.8 2.3 %all-to-all-done.2 = f32[4,144,128]{2,1,0:T(8,128)S(1)} async-done(((f32[4,144,128]{2,1,0:T(8,128)}), f32[4,144,128]{2,1,0:T(8,128)S(1)}, u32[]{:S(2)}, u32[]{:S(2)}) %all-to-all-start.2) | async-done | bytes 294944 | tf_op jit(solution)/shard_map/all_to_all | solution.py:26
  109.4 17.8 %all_to_all.30 = bf16[16,40,128]{2,1,0:T(8,128)(2,1)S(1)} all-to-all(bf16[16,40,128]{2,1,0:T(8,128)(2,1)S(1)} %bitcast.96), channel_id=1, replica_groups=mesh['y'=4,'zl'=8,'zh'=2,'x'=4,'c'=2] {'zh','zl'}, dimensions={0} | all-to-all | bytes 327680 | tf_op jit(solution)/shard_map/all_to_all | solution.py:26
  127.3 14.1 %all_to_all.31 = bf16[8,40,128]{2,1,0:T(8,128)(2,1)S(1)} all-to-all(bf16[8,40,128]{2,1,0:T(8,128)(2,1)S(1)} %broadcast_in_dim.96), channel_id=1, replica_groups=mesh['y'=4,'zl'=8,'zh'=2,'x'=4,'c'=2] {'zl'}, dimensions={0} | all-to-all | bytes 163840 | tf_op jit(solution)/shard_map/all_to_all | solution.py:26
  141.4 0.8 broadcast_in_dim.98
  142.2 3.5 %all-to-all-start.5 = ((bf16[4,320,128]{2,1,0:T(8,128)(2,1)}), bf16[4,320,128]{2,1,0:T(8,128)(2,1)S(1)}, u32[]{:S(2)}, u32[]{:S(2)}) async-start(bf16[4,320,128]{2,1,0:T(8,128)(2,1)} %broadcast_in_dim.98), calls=%async_computation.5 | async-start | bytes 655360 | tf_op jit(solution)/shard_map/all_to_all | solution.py:26
  145.8 6.8 %all-to-all-done.5 = bf16[4,320,128]{2,1,0:T(8,128)(2,1)S(1)} async-done(((bf16[4,320,128]{2,1,0:T(8,128)(2,1)}), bf16[4,320,128]{2,1,0:T(8,128)(2,1)S(1)}, u32[]{:S(2)}, u32[]{:S(2)}) %all-to-all-start.5) | async-done | bytes 327712 | tf_op jit(solution)/shard_map/all_to_all | solution.py:26
  152.8 0.9 fusion.27
  153.7 6.0 %half_product.3 = (bf16[192,512]{1,0:T(8,128)(2,1)}, bf16[192,512]{1,0:T(8,128)(2,1)}, bf16[192,512]{1,0:T(8,128)(2,1)}, bf16[192,512]{1,0:T(8,128)(2,1)}) custom-call(s32[1]{0:T(128)} %bitcast.25.half, bf16[768,2048]{1,0:T(8,128)(2,1)} %bitcast.69, bf16[16,512,256]{2,1,0:T(8,128)(2,1)} %bitcast.71), custom_call_target="tpu_custom_call" | custom-call | flops 1610612736 | bytes 6029312 | tf_op jit(solution)/shard_map/half_product/pallas_call | solution.py:68
  159.6 2.5 %collective-permute-start.14 = (bf16[192,512]{1,0:T(8,128)(2,1)}, bf16[192,512]{1,0:T(8,128)(2,1)S(1)}, u32[]{:S(2)}, u32[]{:S(2)}) collective-permute-start(bf16[192,512]{1,0:T(8,128)(2,1)} %get-tuple-element.27), channel_id=1, source_target_pairs={{0,128},{128,256},{256,384},{384,0},{1,129},{129,257},{257,385},{3... | collective-permute-start | bytes 589832 | tf_op jit(solution)/shard_map/ppermute | solution.py:36
  162.1 4.0 %collective-permute-start.13 = (bf16[192,512]{1,0:T(8,128)(2,1)}, bf16[192,512]{1,0:T(8,128)(2,1)S(1)}, u32[]{:S(2)}, u32[]{:S(2)}) collective-permute-start(bf16[192,512]{1,0:T(8,128)(2,1)} %get-tuple-element.26), channel_id=1, source_target_pairs={{0,256},{128,384},{256,0},{384,128},{1,257},{129,385},{257,1},{385... | collective-permute-start | bytes 589832 | tf_op jit(solution)/shard_map/ppermute | solution.py:36
  166.1 2.5 %collective-permute-start.12 = (bf16[192,512]{1,0:T(8,128)(2,1)}, bf16[192,512]{1,0:T(8,128)(2,1)S(1)}, u32[]{:S(2)}, u32[]{:S(2)}) collective-permute-start(bf16[192,512]{1,0:T(8,128)(2,1)} %get-tuple-element.25), channel_id=1, source_target_pairs={{0,384},{128,0},{256,128},{384,256},{1,385},{129,1},{257,129},{385... | collective-permute-start | bytes 589832 | tf_op jit(solution)/shard_map/ppermute | solution.py:36
  168.6 0.6 slice_bitcast_fusion.4
  169.2 6.0 %half_product.2 = (bf16[192,512]{1,0:T(8,128)(2,1)}, bf16[192,512]{1,0:T(8,128)(2,1)}, bf16[192,512]{1,0:T(8,128)(2,1)}, bf16[192,512]{1,0:T(8,128)(2,1)}) custom-call(s32[1]{0:T(128)} %bitcast.half, bf16[768,2048]{1,0:T(8,128)(2,1)} %bitcast.70, bf16[16,512,256]{2,1,0:T(8,128)(2,1)} %bitcast.72), custom_call_target="tpu_custom_call" | custom-call | flops 1610612736 | bytes 6029312 | tf_op jit(solution)/shard_map/half_product/pallas_call | solution.py:68
  175.2 3.3 %collective-permute-start.11 = (bf16[192,512]{1,0:T(8,128)(2,1)}, bf16[192,512]{1,0:T(8,128)(2,1)S(1)}, u32[]{:S(2)}, u32[]{:S(2)}) collective-permute-start(bf16[192,512]{1,0:T(8,128)(2,1)} %get-tuple-element.23), channel_id=1, source_target_pairs={{0,128},{128,256},{256,384},{384,0},{1,129},{129,257},{257,385},{3... | collective-permute-start | bytes 589832 | tf_op jit(solution)/shard_map/ppermute | solution.py:36
  178.5 3.4 %collective-permute-start.10 = (bf16[192,512]{1,0:T(8,128)(2,1)}, bf16[192,512]{1,0:T(8,128)(2,1)S(1)}, u32[]{:S(2)}, u32[]{:S(2)}) collective-permute-start(bf16[192,512]{1,0:T(8,128)(2,1)} %get-tuple-element.22), channel_id=1, source_target_pairs={{0,256},{128,384},{256,0},{384,128},{1,257},{129,385},{257,1},{385... | collective-permute-start | bytes 589832 | tf_op jit(solution)/shard_map/ppermute | solution.py:36
  182.0 4.5 %collective-permute-start.9 = (bf16[192,512]{1,0:T(8,128)(2,1)}, bf16[192,512]{1,0:T(8,128)(2,1)S(1)}, u32[]{:S(2)}, u32[]{:S(2)}) collective-permute-start(bf16[192,512]{1,0:T(8,128)(2,1)} %get-tuple-element.21), channel_id=1, source_target_pairs={{0,384},{128,0},{256,128},{384,256},{1,385},{129,1},{257,129},{385... | collective-permute-start | bytes 589832 | tf_op jit(solution)/shard_map/ppermute | solution.py:36
  186.8 9.9 %collective-permute-start.15 = (bf16[192,512]{1,0:T(8,128)(2,1)S(1)}, bf16[192,512]{1,0:T(8,128)(2,1)S(1)}, u32[]{:S(2)}, u32[]{:S(2)}) collective-permute-start(bf16[192,512]{1,0:T(8,128)(2,1)S(1)} %add_convert_fusion), channel_id=1, source_target_pairs={{0,8},{8,0},{1,9},{9,1},{2,10},{10,2},{3,11},{11,3},{4,12},{12,4},... | collective-permute-start | bytes 589832 | tf_op jit(solution)/shard_map/ppermute | solution.py:52
  196.7 1.2 add_convert_fusion.1
  197.9 12.7 %collective-permute-done.15 = bf16[192,512]{1,0:T(8,128)(2,1)S(1)} collective-permute-done((bf16[192,512]{1,0:T(8,128)(2,1)S(1)}, bf16[192,512]{1,0:T(8,128)(2,1)S(1)}, u32[]{:S(2)}, u32[]{:S(2)}) %collective-permute-start.15) | collective-permute-done | bytes 196640 | tf_op jit(solution)/shard_map/ppermute | solution.py:52
  210.5 0.9 bitcast_select_fusion
  (71 shorter events, 3.3 us)
Async XLA Ops:
  7.2 2.0 copy-start
  7.2 19.4 %copy-start.1 = (bf16[24,8192]{1,0:T(8,128)(2,1)S(1)}, bf16[24,8192]{1,0:T(8,128)(2,1)}, u32[]{:S(2)}) copy-start(bf16[24,8192]{1,0:T(8,128)(2,1)} %param.9) | copy-start | bytes 1179652
  7.2 146.5 %all-gather.3.cloned.1.call-start = ((), (), s32[]{:S(2)}) async-start(), calls=%async_computation.6 | async-start | bytes 4456448 | tf_op jit(solution)/shard_map/all_gather | solution.py:110
  11.0 31.8 %collective-permute-start.7 = (bf16[48,896]{1,0:T(8,128)(2,1)S(1)}, bf16[48,896]{1,0:T(8,128)(2,1)S(1)}, u32[]{:S(2)}, u32[]{:S(2)}) collective-permute-start(bf16[48,896]{1,0:T(8,128)(2,1)S(1)} %pad_maximum_fusion.9), channel_id=1, source_target_pairs={{0,8},{8,0},{1,9},{9,1},{2,10},{10,2},{3,11},{11,3},{4,12},{12,4},... | collective-permute-start | bytes 258056 | tf_op jit(solution)/shard_map/ppermute | solution.py:52
  26.7 16.3 %collective-permute-start.2 = (bf16[24,2048]{1,0:T(8,128)(2,1)S(1)}, bf16[24,2048]{1,0:T(8,128)(2,1)S(1)}, u32[]{:S(2)}, u32[]{:S(2)}) collective-permute-start(bf16[24,2048]{1,0:T(8,128)(2,1)S(1)} %get-tuple-element.40), channel_id=1, source_target_pairs={{0,384},{128,0},{256,128},{384,256},{1,385},{129,1},{257,129},{385... | collective-permute-start | bytes 294920 | tf_op jit(solution)/shard_map/ppermute | solution.py:36
  31.7 11.4 %collective-permute-start.1 = (bf16[24,2048]{1,0:T(8,128)(2,1)S(1)}, bf16[24,2048]{1,0:T(8,128)(2,1)S(1)}, u32[]{:S(2)}, u32[]{:S(2)}) collective-permute-start(bf16[24,2048]{1,0:T(8,128)(2,1)S(1)} %get-tuple-element.41), channel_id=1, source_target_pairs={{0,256},{128,384},{256,0},{384,128},{1,257},{129,385},{257,1},{385... | collective-permute-start | bytes 294920 | tf_op jit(solution)/shard_map/ppermute | solution.py:36
  34.2 8.8 %collective-permute-start = (bf16[24,2048]{1,0:T(8,128)(2,1)S(1)}, bf16[24,2048]{1,0:T(8,128)(2,1)S(1)}, u32[]{:S(2)}, u32[]{:S(2)}) collective-permute-start(bf16[24,2048]{1,0:T(8,128)(2,1)S(1)} %get-tuple-element.42), channel_id=1, source_target_pairs={{0,128},{128,256},{256,384},{384,0},{1,129},{129,257},{257,385},{3... | collective-permute-start | bytes 294920 | tf_op jit(solution)/shard_map/ppermute | solution.py:36
  37.1 5.9 %copy-start.4 = (bf16[16,512]{1,0:T(8,128)(2,1)S(1)}, bf16[16,512]{1,0:T(8,128)(2,1)}, u32[]{:S(2)}) copy-start(bf16[16,512]{1,0:T(8,128)(2,1)} %param.15) | copy-start | bytes 49156
  38.6 15.3 %all-to-all-start = ((bf16[8,24,1024]{2,1,0:T(8,128)(2,1)}), bf16[8,24,1024]{2,1,0:T(8,128)(2,1)S(1)}, u32[]{:S(2)}, u32[]{:S(2)}) async-start(bf16[8,24,1024]{2,1,0:T(8,128)(2,1)} %reshape.112), calls=%async_computation | async-start | bytes 786432 | tf_op jit(solution)/shard_map/all_to_all | solution.py:26
  43.1 15.6 %copy-start.5 = (s32[32]{0:T(128)S(1)}, s32[32]{0:T(128)}, u32[]{:S(2)}) copy-start(s32[32]{0:T(128)} %param.17) | copy-start | bytes 388
  43.1 16.1 %collective-permute-start.5 = (bf16[96,2048]{1,0:T(8,128)(2,1)S(1)}, bf16[96,2048]{1,0:T(8,128)(2,1)S(1)}, u32[]{:S(2)}, u32[]{:S(2)}) collective-permute-start(bf16[96,2048]{1,0:T(8,128)(2,1)S(1)} %bitcast.76), channel_id=1, source_target_pairs={{0,6},{2,0},{4,2},{6,4},{1,7},{3,1},{5,3},{7,5},{8,14},{10,8},{12,... | collective-permute-start | bytes 1179656 | tf_op jit(solution)/shard_map/ppermute | solution.py:36
  48.3 15.4 %collective-permute-start.4 = (bf16[96,2048]{1,0:T(8,128)(2,1)S(1)}, bf16[96,2048]{1,0:T(8,128)(2,1)S(1)}, u32[]{:S(2)}, u32[]{:S(2)}) collective-permute-start(bf16[96,2048]{1,0:T(8,128)(2,1)S(1)} %bitcast.77), channel_id=1, source_target_pairs={{0,4},{2,6},{4,0},{6,2},{1,5},{3,7},{5,1},{7,3},{8,12},{10,14},{12... | collective-permute-start | bytes 1179656 | tf_op jit(solution)/shard_map/ppermute | solution.py:36
  51.1 20.8 %collective-permute-start.3 = (bf16[96,2048]{1,0:T(8,128)(2,1)S(1)}, bf16[96,2048]{1,0:T(8,128)(2,1)S(1)}, u32[]{:S(2)}, u32[]{:S(2)}) collective-permute-start(bf16[96,2048]{1,0:T(8,128)(2,1)S(1)} %bitcast.78), channel_id=1, source_target_pairs={{0,2},{2,4},{4,6},{6,0},{1,3},{3,5},{5,7},{7,1},{8,10},{10,12},{12... | collective-permute-start | bytes 1179656 | tf_op jit(solution)/shard_map/ppermute | solution.py:36
  55.0 22.3 %all-to-all-start.1 = ((f32[8,48,384]{2,1,0:T(8,128)}), f32[8,48,384]{2,1,0:T(8,128)S(1)}, u32[]{:S(2)}, u32[]{:S(2)}) async-start(f32[8,48,384]{2,1,0:T(8,128)} %broadcast_in_dim.91), calls=%async_computation.1 | async-start | bytes 1179648 | tf_op jit(solution)/shard_map/all_to_all | solution.py:26
  71.9 5.5 %copy-start.3 = (bf16[16,512]{1,0:T(8,128)(2,1)S(1)}, bf16[16,512]{1,0:T(8,128)(2,1)}, u32[]{:S(2)}) copy-start(bf16[16,512]{1,0:T(8,128)(2,1)} %param.14) | copy-start | bytes 49156
  73.2 29.0 %collective-permute-start.6 = (bf16[4,96,2048]{2,1,0:T(8,128)(2,1)}, bf16[4,96,2048]{2,1,0:T(8,128)(2,1)}, u32[]{:S(2)}, u32[]{:S(2)}) collective-permute-start(bf16[4,96,2048]{2,1,0:T(8,128)(2,1)} %pad_maximum_fusion.1), channel_id=1, source_target_pairs={{0,1},{1,0},{2,3},{3,2},{4,5},{5,4},{6,7},{7,6},{8,9},{9,8},{10,11... | collective-permute-start | bytes 4718600 | tf_op jit(solution)/shard_map/ppermute | solution.py:36
  77.5 18.7 %collective-permute-start.8 = (bf16[48,704]{1,0:T(8,128)(2,1)S(1)}, bf16[48,704]{1,0:T(8,128)(2,1)S(1)}, u32[]{:S(2)}, u32[]{:S(2)}) collective-permute-start(bf16[48,704]{1,0:T(8,128)(2,1)S(1)} %maximum_maximum_fusion), channel_id=1, source_target_pairs={{0,8},{8,0},{1,9},{9,1},{2,10},{10,2},{3,11},{11,3},{4,12},{12,4},... | collective-permute-start | bytes 202760 | tf_op jit(solution)/shard_map/ppermute | solution.py:52
  97.2 11.9 %all-to-all-start.2 = ((f32[4,144,128]{2,1,0:T(8,128)}), f32[4,144,128]{2,1,0:T(8,128)S(1)}, u32[]{:S(2)}, u32[]{:S(2)}) async-start(f32[4,144,128]{2,1,0:T(8,128)} %pad_maximum_fusion.7), calls=%async_computation.2 | async-start | bytes 589824 | tf_op jit(solution)/shard_map/all_to_all | solution.py:26
  142.2 10.5 %all-to-all-start.5 = ((bf16[4,320,128]{2,1,0:T(8,128)(2,1)}), bf16[4,320,128]{2,1,0:T(8,128)(2,1)S(1)}, u32[]{:S(2)}, u32[]{:S(2)}) async-start(bf16[4,320,128]{2,1,0:T(8,128)(2,1)} %broadcast_in_dim.98), calls=%async_computation.5 | async-start | bytes 655360 | tf_op jit(solution)/shard_map/all_to_all | solution.py:26
  159.6 22.3 %collective-permute-start.14 = (bf16[192,512]{1,0:T(8,128)(2,1)}, bf16[192,512]{1,0:T(8,128)(2,1)S(1)}, u32[]{:S(2)}, u32[]{:S(2)}) collective-permute-start(bf16[192,512]{1,0:T(8,128)(2,1)} %get-tuple-element.27), channel_id=1, source_target_pairs={{0,128},{128,256},{256,384},{384,0},{1,129},{129,257},{257,385},{3... | collective-permute-start | bytes 589832 | tf_op jit(solution)/shard_map/ppermute | solution.py:36
  162.1 24.4 %collective-permute-start.13 = (bf16[192,512]{1,0:T(8,128)(2,1)}, bf16[192,512]{1,0:T(8,128)(2,1)S(1)}, u32[]{:S(2)}, u32[]{:S(2)}) collective-permute-start(bf16[192,512]{1,0:T(8,128)(2,1)} %get-tuple-element.26), channel_id=1, source_target_pairs={{0,256},{128,384},{256,0},{384,128},{1,257},{129,385},{257,1},{385... | collective-permute-start | bytes 589832 | tf_op jit(solution)/shard_map/ppermute | solution.py:36
  166.1 20.4 %collective-permute-start.12 = (bf16[192,512]{1,0:T(8,128)(2,1)}, bf16[192,512]{1,0:T(8,128)(2,1)S(1)}, u32[]{:S(2)}, u32[]{:S(2)}) collective-permute-start(bf16[192,512]{1,0:T(8,128)(2,1)} %get-tuple-element.25), channel_id=1, source_target_pairs={{0,384},{128,0},{256,128},{384,256},{1,385},{129,1},{257,129},{385... | collective-permute-start | bytes 589832 | tf_op jit(solution)/shard_map/ppermute | solution.py:36
  169.2 17.3 %copy-start.2 = (bf16[192,512]{1,0:T(8,128)(2,1)S(1)}, bf16[192,512]{1,0:T(8,128)(2,1)}, u32[]{:S(2)}) copy-start(bf16[192,512]{1,0:T(8,128)(2,1)} %get-tuple-element.24) | copy-start | bytes 589828
  175.2 21.5 %collective-permute-start.11 = (bf16[192,512]{1,0:T(8,128)(2,1)}, bf16[192,512]{1,0:T(8,128)(2,1)S(1)}, u32[]{:S(2)}, u32[]{:S(2)}) collective-permute-start(bf16[192,512]{1,0:T(8,128)(2,1)} %get-tuple-element.23), channel_id=1, source_target_pairs={{0,128},{128,256},{256,384},{384,0},{1,129},{129,257},{257,385},{3... | collective-permute-start | bytes 589832 | tf_op jit(solution)/shard_map/ppermute | solution.py:36
  178.5 18.2 %collective-permute-start.10 = (bf16[192,512]{1,0:T(8,128)(2,1)}, bf16[192,512]{1,0:T(8,128)(2,1)S(1)}, u32[]{:S(2)}, u32[]{:S(2)}) collective-permute-start(bf16[192,512]{1,0:T(8,128)(2,1)} %get-tuple-element.22), channel_id=1, source_target_pairs={{0,256},{128,384},{256,0},{384,128},{1,257},{129,385},{257,1},{385... | collective-permute-start | bytes 589832 | tf_op jit(solution)/shard_map/ppermute | solution.py:36
  182.0 14.7 %collective-permute-start.9 = (bf16[192,512]{1,0:T(8,128)(2,1)}, bf16[192,512]{1,0:T(8,128)(2,1)S(1)}, u32[]{:S(2)}, u32[]{:S(2)}) collective-permute-start(bf16[192,512]{1,0:T(8,128)(2,1)} %get-tuple-element.21), channel_id=1, source_target_pairs={{0,384},{128,0},{256,128},{384,256},{1,385},{129,1},{257,129},{385... | collective-permute-start | bytes 589832 | tf_op jit(solution)/shard_map/ppermute | solution.py:36
  186.8 23.7 %collective-permute-start.15 = (bf16[192,512]{1,0:T(8,128)(2,1)S(1)}, bf16[192,512]{1,0:T(8,128)(2,1)S(1)}, u32[]{:S(2)}, u32[]{:S(2)}) collective-permute-start(bf16[192,512]{1,0:T(8,128)(2,1)S(1)} %add_convert_fusion), channel_id=1, source_target_pairs={{0,8},{8,0},{1,9},{9,1},{2,10},{10,2},{3,11},{11,3},{4,12},{12,4},... | collective-permute-start | bytes 589832 | tf_op jit(solution)/shard_map/ppermute | solution.py:52
Sparse Core Ops, SparseCore 0:
  26.0 77.5 all-gather.2
